TPU v7x, 256 devices: a whole 4x4x8 slice. The times are simulated.
256 devices in a mesh: dp: 8 (over z), tensor: 32 (over x, y, core).
Axes of the slice: x: 4, y: 4, z: 8, core: 2. Of those that a mesh axis runs over, the one named last changes fastest.
Arguments:
- activations: bfloat16 [2048, 27648], P('dp', 'tensor'), may hold values from -6 to 6
- left_factor: float32 [216, 216], replicated, may hold values from -2 to 3, as said below
- right_factor: float32 [128, 128], replicated, may hold values from -2 to 3, as said below
- clip_scale: float32 [128, 216], replicated, may hold values from 0.5 to 3
- weight_rows: bfloat16 [27648, 5120], P('tensor'), may hold values from -0.0390625 to 0.0390625
- target: bfloat16 [2048, 5120], P('dp'), may hold values from -6 to 6
Outputs:
- grad_left: float32 [216, 216], replicated
- grad_right: float32 [128, 128], replicated
- grad_input: float32 [2048, 27648], P('dp', 'tensor')
Inputs may be any that keep to these rules, and one draw needn't show every extreme that they name: `left_factor`: the identity plus independent entries of order one over the square root of 216. `right_factor`: the identity plus independent entries of order one over the square root of 128.
All inputs are finite; a program needn't handle non-finite values.
Results may differ from a plain program's by a relative error of at most 0.007.
Values may be sent and summed in bfloat16 or wider, within the bound.
No kernel may reach another device: no remote copies, remote signals or barrier semaphores. Data moves between devices by JAX's collectives and lax.ppermute only.
A program may use at most 64 MiB of HBM per device.

v0:
```python
import jax
import jax.numpy as jnp
from jax import lax
from jax.sharding import Mesh
from jax.sharding import PartitionSpec as P

TENSOR = ("tensor_0", "tensor_1", "tensor_2")


def split_up(array, dim, size):
    lengths = array.shape
    blocks = array.reshape(*lengths[:dim], size, lengths[dim] // size, *lengths[dim + 1 :])
    return jnp.moveaxis(blocks, dim, 0)


def summed_on_arrival(array, axis, dim):
    size = lax.axis_size(axis)
    blocks = lax.all_to_all(split_up(array, dim, size), axis, 0, 0, tiled=True)
    return jnp.sum(blocks.astype(jnp.float32), axis=0)


def summed_rows(array, axes, dim):
    far, near = axes
    blocks = split_up(array, dim, lax.axis_size(far))
    nearer = summed_on_arrival(blocks, near, dim + 1)
    arrived = lax.all_to_all(
        nearer.astype(jnp.bfloat16), far, split_axis=0, concat_axis=0, tiled=True
    )
    return arrived.astype(jnp.float32).sum(axis=0)


def copy_for_each(array, axis):
    size = lax.axis_size(axis)
    return lax.all_to_all(
        jnp.broadcast_to(array[None], (size, *array.shape)), axis, 0, 0, tiled=True
    )


def joined_along(blocks, dim):
    blocks = jnp.moveaxis(blocks, 0, dim)
    lengths = blocks.shape
    return blocks.reshape(*lengths[:dim], lengths[dim] * lengths[dim + 1], *lengths[dim + 2 :])


def whole_of(array, axes, dim):
    far, near = axes
    blocks = copy_for_each(copy_for_each(array, far), near)
    return joined_along(blocks.swapaxes(0, 1).reshape(-1, *array.shape), dim)


def sum_at_owner(array, axis, dim):
    size = lax.axis_size(axis)
    blocks = lax.all_to_all(split_up(array, dim, size), axis, 0, 0, tiled=True)
    return jnp.sum(blocks, axis=0)


def sum_by_axis(array, axes, dim):
    far, near = axes
    blocks = split_up(array, dim, lax.axis_size(far))
    nearer = sum_at_owner(blocks, near, dim + 1)
    arrived = lax.all_to_all(nearer, far, split_axis=0, concat_axis=0, tiled=True)
    return arrived.sum(axis=0)


def rows_for(lines, size):
    spare = -len(lines) % size
    return jnp.pad(lines, [(0, spare)] + [(0, 0)] * (lines.ndim - 1))


def total_of(array, axes):
    own = sum_by_axis(rows_for(array, lax.axis_size(axes[0]) * lax.axis_size(axes[1])), axes, 0)
    whole = whole_of(own, axes, 0)
    return whole[: len(array)].reshape(array.shape)


def packed_total(arrays, axis):
    line, at, done = (jnp.concatenate([a.reshape(-1) for a in arrays]), 0, [])
    total = total_of(line, axis)
    for a in arrays:
        done.append(total[at : at + a.size].reshape(a.shape))
        at += a.size
    return tuple(done)


def local(activations, left_factor, right_factor, clip_scale, weight_rows, target):
    highest = lax.Precision.HIGHEST
    tok_rows = activations.shape[0]
    width_left = left_factor.shape[0]
    local_right = activations.shape[1] // width_left
    inputs = activations.reshape(tok_rows, local_right, width_left)
    moved = lax.all_to_all(inputs, TENSOR, split_axis=0, concat_axis=1, tiled=True)
    mixed = jnp.einsum("tji,ik->tjk", moved.astype(jnp.float32), left_factor, precision=highest)
    rotated = jnp.einsum("jl,tjk->tlk", right_factor, mixed, precision=highest)
    bounded = jnp.tanh(rotated / clip_scale)
    clipped = (clip_scale * bounded).astype(jnp.bfloat16)
    clipped_back = lax.all_to_all(clipped, TENSOR, split_axis=1, concat_axis=0, tiled=True)
    partial_out = jnp.dot(
        clipped_back.reshape(tok_rows, -1), weight_rows, preferred_element_type=jnp.float32
    )
    share = summed_rows(partial_out.astype(jnp.bfloat16), (("tensor_0", "tensor_1"), "tensor_2"), 1)
    columns = share.shape[1]
    start = lax.axis_index(TENSOR) * columns
    own_target = lax.dynamic_slice_in_dim(target, start, columns, 1)
    grad_share = (share - own_target.astype(jnp.float32)).astype(jnp.bfloat16)
    out_grad = whole_of(grad_share, (("tensor_0", "tensor_1"), "tensor_2"), 1)
    clipped_grad = lax.dot_general(
        out_grad, weight_rows, (((1,), (1,)), ((), ())), preferred_element_type=jnp.float32
    )
    clipped_grad = clipped_grad.reshape(tok_rows, local_right, width_left)
    grad_owned = lax.all_to_all(
        clipped_grad.astype(jnp.bfloat16), TENSOR, split_axis=0, concat_axis=1, tiled=True
    ).astype(clipped_grad.dtype)
    rotated_grad = grad_owned * (1.0 - bounded * bounded)
    mixed_grad = jnp.einsum("jl,tlk->tjk", right_factor, rotated_grad, precision=highest)
    right_part = jnp.einsum("tjk,tlk->jl", mixed, rotated_grad, precision=highest)
    grad_back = lax.all_to_all(
        mixed_grad.astype(jnp.bfloat16), TENSOR, split_axis=1, concat_axis=0, tiled=True
    ).astype(mixed_grad.dtype)
    input_grad = jnp.einsum("tjk,ik->tji", grad_back, left_factor, precision=highest).reshape(
        tok_rows, -1
    )
    left_part = jnp.einsum("tji,tjk->ik", inputs.astype(jnp.float32), grad_back, precision=highest)
    left_sum, right_sum = packed_total(
        (left_part, right_part), (("dp", "tensor_0"), ("tensor_1", "tensor_2"))
    )
    return (left_sum, right_sum, input_grad)


def solution(mesh):
    torus = Mesh(
        mesh.devices.reshape(mesh.shape["dp"], 4, 4, 2), ("dp", "tensor_0", "tensor_1", "tensor_2")
    )
    placed = (P("dp", TENSOR), P(), P(), P(), P(TENSOR, None), P("dp", None))
    return jax.shard_map(
        local, mesh=torus, in_specs=placed, out_specs=(P(), P(), P("dp", TENSOR)), check_vma=False
    )
```

profile of v0, /device:TPU:1, one launch (start us, length us, event | category | flops | bytes accessed | tf_op | source)
XLA Modules:
  0.0 227.2 jit_solution(426309295226351361)
XLA Ops:
  0.7 1.5 copy.94
  2.2 20.1 %all_to_all.105 = bf16[256,4,216]{2,1,0:T(4,128)(2,1)S(1)} all-to-all(bf16[256,4,216]{2,1,0:T(4,128)(2,1)S(1)} %copy.94), channel_id=1, replica_groups=mesh['dp'=8,'tensor_0'=4,'tensor_1'=4,'tensor_2'=2] {'tensor_0','tensor_..., dimensions={0} | all-to-all | bytes 884736 | tf_op jit(solution)/shard_map/all_to_all | solution.py:91
  24.1 2.0 multiply_convert_fusion
  26.0 1.4 copy.99
  27.5 15.0 %all_to_all.106 = bf16[8,128,216]{2,0,1:T(8,128)(2,1)S(1)} all-to-all(bf16[8,128,216]{2,0,1:T(8,128)(2,1)S(1)} %copy.99), channel_id=1, replica_groups=mesh['dp'=8,'tensor_0'=4,'tensor_1'=4,'tensor_2'=2] {'tensor_0','tensor_..., dimensions={1} | all-to-all | bytes 884736 | tf_op jit(solution)/shard_map/all_to_all | solution.py:96
  42.8 1.2 reshape.60
  43.9 8.1 %convolution_convert_fusion = bf16[256,5120]{1,0:T(8,128)(2,1)} fusion(bf16[256,864]{1,0:T(8,128)(2,1)} %reshape.60, bf16[864,5120]{1,0:T(8,128)(2,1)} %param.10), kind=kOutput, calls=%fused_computation | convolution fusion | flops 2266234880 | bytes 11911168 | tf_op jit(solution)/shard_map/dot_general | solution.py:97
  52.0 4.4 %copy.101 = bf16[256,5120]{0,1:T(8,128)(2,1)} copy(bf16[256,5120]{1,0:T(8,128)(2,1)} %convolution_convert_fusion) | data formatting | bytes 5242880 | tf_op jit(solution)/shard_map/convert_element_type | solution.py:100
  56.4 1.9 copy.102
  58.3 6.4 %all_to_all.107 = bf16[2,16,256,160]{2,3,1,0:T(8,128)(2,1)} all-to-all(bf16[2,16,256,160]{2,3,1,0:T(8,128)(2,1)S(1)} %copy.102), channel_id=1, replica_groups=mesh['dp'=8,'tensor_0'=4,'tensor_1'=4,'tensor_2'=2] {'tensor_2'}, dimensions={0} | all-to-all | bytes 5242880 | tf_op jit(solution)/shard_map/all_to_all | solution.py:18
  64.7 3.7 %reduce_sum.39 = bf16[16,256,160]{1,2,0:T(8,128)(2,1)} reduce(bf16[2,16,256,160]{2,3,1,0:T(8,128)(2,1)} %all_to_all.107, bf16[]{:T(256)} %constant.10.clone.1), dimensions={0}, to_apply=%region_0.0 | reduce | flops 655360 | bytes 3932162 | tf_op jit(solution)/shard_map/reduce_sum | solution.py:19
  68.4 4.5 %all-to-all-start.3 = ((bf16[16,256,160]{1,2,0:T(8,128)(2,1)}), bf16[16,256,160]{1,2,0:T(8,128)(2,1)}, u32[]{:S(2)}, u32[]{:S(2)}) async-start(bf16[16,256,160]{1,2,0:T(8,128)(2,1)} %reduce_sum.39), calls=%async_computation.3 | async-start | bytes 2621440 | tf_op jit(solution)/shard_map/all_to_all | solution.py:26
  73.2 20.0 %all-to-all-done.3 = bf16[16,256,160]{1,2,0:T(8,128)(2,1)} async-done(((bf16[16,256,160]{1,2,0:T(8,128)(2,1)}), bf16[16,256,160]{1,2,0:T(8,128)(2,1)}, u32[]{:S(2)}, u32[]{:S(2)}) %all-to-all-start.3) | async-done | bytes 1310752 | tf_op jit(solution)/shard_map/all_to_all | solution.py:26
  93.2 1.5 convert_reduce_fusion
  94.8 20.8 %all_to_all.108 = bf16[16,256,160]{1,2,0:T(8,128)(2,1)S(1)} all-to-all(bf16[16,256,160]{1,2,0:T(8,128)(2,1)S(1)} %broadcast_in_dim.10), channel_id=1, replica_groups=mesh['dp'=8,'tensor_0'=4,'tensor_1'=4,'tensor_2'=2] {'tensor_0','tensor_1'}, dimensions={0} | all-to-all | bytes 2621440 | tf_op jit(solution)/shard_map/all_to_all | solution.py:34
  116.0 9.1 %all_to_all.109 = bf16[2,16,256,160]{2,3,1,0:T(8,128)(2,1)S(1)} all-to-all(bf16[2,16,256,160]{2,3,1,0:T(8,128)(2,1)S(1)} %broadcast_in_dim.11), channel_id=1, replica_groups=mesh['dp'=8,'tensor_0'=4,'tensor_1'=4,'tensor_2'=2] {'tensor_2'}, dimensions={0} | all-to-all | bytes 5242880 | tf_op jit(solution)/shard_map/all_to_all | solution.py:34
  125.3 3.2 %convolution_convert_fusion.2 = bf16[256,4,216]{0,2,1:T(8,128)(2,1)} fusion(bf16[256,5120,1]{0,1,2:T(8,128)(2,1)S(1)} %bitcast.87, bf16[4,216,5120]{2,1,0:T(8,128)(2,1)S(1)} %bitcast.99), kind=kOutput, calls=%fused_computation.7 | convolution fusion | flops 2265145344 | bytes 11911168 | tf_op jit(solution)/shard_map/dot_general | solution.py:106
  128.5 1.3 copy.107
  129.8 15.5 %all_to_all.110 = bf16[256,4,216]{2,1,0:T(4,128)(2,1)S(1)} all-to-all(bf16[256,4,216]{2,1,0:T(4,128)(2,1)S(1)} %copy.107), channel_id=1, replica_groups=mesh['dp'=8,'tensor_0'=4,'tensor_1'=4,'tensor_2'=2] {'tensor_0','tensor_..., dimensions={0} | all-to-all | bytes 884736 | tf_op jit(solution)/shard_map/all_to_all | solution.py:110
  146.5 1.6 copy.110
  148.1 2.8 %fusion.2 = bf16[8,128,216]{1,2,0:T(8,128)(2,1)} fusion(f32[8,128,216]{1,2,0:T(8,128)S(1)} %copy.110, f32[8,128,216]{1,2,0:T(8,128)} %get-tuple-element.4, f32[128,128]{1,0:T(8,128)} %param.8), kind=kOutput, calls=%fused_computation.8 | convolution fusion | flops 340623360 | bytes 2277376 | tf_op jit(solution)/shard_map/jl,tlk->tjk/dot_general | solution.py:114
  150.9 2.2 copy.111
  153.1 4.4 %all-to-all-start.7 = ((bf16[8,128,216]{2,0,1:T(8,128)(2,1)}), bf16[8,128,216]{2,0,1:T(8,128)(2,1)}, u32[]{:S(2)}, u32[]{:S(2)}) async-start(bf16[8,128,216]{2,0,1:T(8,128)(2,1)} %copy.111), calls=%async_computation.7 | async-start | bytes 1048576 | tf_op jit(solution)/shard_map/all_to_all | solution.py:116
  157.5 3.7 %convolution_bitcast_fusion = f32[16384]{0:T(1024)} fusion(f32[8,128,216]{1,2,0:T(8,128)} %copy-done.1, f32[8,128,216]{1,2,0:T(8,128)S(1)} %copy.110, f32[8,128,216]{1,2,0:T(8,128)} %get-tuple-element.4), kind=kOutput, calls=%fused_computation.2 | convolution fusion | flops 340402176 | bytes 2719744 | tf_op jit(solution)/shard_map/tjk,tlk->jl/dot_general | solution.py:115
  161.2 7.7 %all-to-all-done.7 = bf16[8,128,216]{2,0,1:T(8,128)(2,1)} async-done(((bf16[8,128,216]{2,0,1:T(8,128)(2,1)}), bf16[8,128,216]{2,0,1:T(8,128)(2,1)}, u32[]{:S(2)}, u32[]{:S(2)}) %all-to-all-start.7) | async-done | bytes 442400 | tf_op jit(solution)/shard_map/all_to_all | solution.py:116
  168.9 1.5 convolution_bitcast_fusion.2
  172.2 9.2 %all_to_all.111 = f32[8,32,247]{2,1,0:T(8,128)S(1)} all-to-all(f32[8,32,247]{2,1,0:T(8,128)S(1)} %copy.115), channel_id=1, replica_groups=mesh['dp'=8,'tensor_0'=4,'tensor_1'=4,'tensor_2'=2] {'tensor_1','tensor_2'}, dimensions={0} | all-to-all | bytes 505856 | tf_op jit(solution)/shard_map/all_to_all | solution.py:53
  181.4 17.7 %all_to_all.112 = f32[32,1,247]{2,1,0:T(1,128)S(1)} all-to-all(f32[32,1,247]{2,1,0:T(1,128)S(1)} %all_to_all.89), channel_id=1, replica_groups=mesh['dp'=8,'tensor_0'=4,'tensor_1'=4,'tensor_2'=2] {'dp','tensor_0'}, dimensions={0} | all-to-all | bytes 63232 | tf_op jit(solution)/shard_map/all_to_all | solution.py:61
  199.2 11.6 %all_to_all.113 = f32[32,1,247]{2,1,0:T(1,128)S(1)} all-to-all(f32[32,1,247]{2,1,0:T(1,128)S(1)} %broadcast_in_dim.12), channel_id=1, replica_groups=mesh['dp'=8,'tensor_0'=4,'tensor_1'=4,'tensor_2'=2] {'dp','tensor_0'}, dimensions={0} | all-to-all | bytes 63232 | tf_op jit(solution)/shard_map/all_to_all | solution.py:34
  211.5 6.9 %all-to-all-start.11 = ((f32[8,32,247]{2,1,0:T(8,128)}), f32[8,32,247]{2,1,0:T(8,128)S(1)}, u32[]{:S(2)}, u32[]{:S(2)}) async-start(f32[8,32,247]{2,1,0:T(8,128)} %broadcast_in_dim.14), calls=%async_computation.11 | async-start | bytes 524288 | tf_op jit(solution)/shard_map/all_to_all | solution.py:34
  218.4 2.6 %fusion.3 = f32[256,4,216]{0,2,1:T(8,128)} fusion(bf16[32,8,4,216]{3,1,2,0:T(8,128)(2,1)} %bitcast.24, f32[216,216]{1,0:T(8,128)S(1)} %copy-done.3), kind=kOutput, calls=%fused_computation.13 | convolution fusion | flops 573308928 | bytes 1513728 | tf_op jit(solution)/shard_map/tjk,ik->tji/dot_general | solution.py:119
  221.0 3.9 %all-to-all-done.11 = f32[8,32,247]{2,1,0:T(8,128)S(1)} async-done(((f32[8,32,247]{2,1,0:T(8,128)}), f32[8,32,247]{2,1,0:T(8,128)S(1)}, u32[]{:S(2)}, u32[]{:S(2)}) %all-to-all-start.11) | async-done | bytes 252960 | tf_op jit(solution)/shard_map/all_to_all | solution.py:34
  (47 shorter events, 9.0 us)
Async XLA Ops:
  0.6 72.3 %copy-start = (bf16[256,5120]{1,0:T(8,128)(2,1)S(1)}, bf16[256,5120]{1,0:T(8,128)(2,1)}, u32[]{:S(2)}) copy-start(bf16[256,5120]{1,0:T(8,128)(2,1)} %param.11) | copy-start | bytes 7864324
  0.6 21.8 %copy-start.2 = (f32[216,216]{1,0:T(8,128)S(1)}, f32[216,216]{1,0:T(8,128)}, u32[]{:S(2)}) copy-start(f32[216,216]{1,0:T(8,128)} %param.7) | copy-start | bytes 559876
  2.1 21.9 %copy-start.4 = (f32[128,128]{1,0:T(8,128)S(1)}, f32[128,128]{1,0:T(8,128)}, u32[]{:S(2)}) copy-start(f32[128,128]{1,0:T(8,128)} %param.8) | copy-start | bytes 196612
  2.2 21.9 %copy-start.5 = (f32[128,216]{0,1:T(8,128)S(1)}, f32[128,216]{0,1:T(8,128)}, u32[]{:S(2)}) copy-start(f32[128,216]{0,1:T(8,128)} %param.9) | copy-start | bytes 331780
  23.2 0.9 copy-start.1
  68.4 56.9 %slice-start = ((s8[8847360]{0:T(1024)(128)(4,1)}), s8[458752]{0:T(1024)(128)(4,1)S(1)}, s32[]{:S(2)}) async-start(s8[8847360]{0:T(1024)(128)(4,1)} %bitcast.97), calls=%async_computation.12 | async-start | bytes 917504
  68.4 24.7 %all-to-all-start.3 = ((bf16[16,256,160]{1,2,0:T(8,128)(2,1)}), bf16[16,256,160]{1,2,0:T(8,128)(2,1)}, u32[]{:S(2)}, u32[]{:S(2)}) async-start(bf16[16,256,160]{1,2,0:T(8,128)(2,1)} %reduce_sum.39), calls=%async_computation.3 | async-start | bytes 2621440 | tf_op jit(solution)/shard_map/all_to_all | solution.py:26
  94.8 30.5 %slice-start.1 = ((s8[8847360]{0:T(1024)(128)(4,1)}), s8[4194304]{0:T(1024)(128)(4,1)S(1)}, s32[]{:S(2)}) async-start(s8[8847360]{0:T(1024)(128)(4,1)} %bitcast.97), calls=%async_computation.13 | async-start | bytes 8388608
  116.0 9.3 %slice-start.2 = ((s8[8847360]{0:T(1024)(128)(4,1)}), s8[4194304]{0:T(1024)(128)(4,1)S(1)}, s32[]{:S(2)}) async-start(s8[8847360]{0:T(1024)(128)(4,1)} %bitcast.97), calls=%async_computation.14 | async-start | bytes 8388608
  153.1 15.8 %all-to-all-start.7 = ((bf16[8,128,216]{2,0,1:T(8,128)(2,1)}), bf16[8,128,216]{2,0,1:T(8,128)(2,1)}, u32[]{:S(2)}, u32[]{:S(2)}) async-start(bf16[8,128,216]{2,0,1:T(8,128)(2,1)} %copy.111), calls=%async_computation.7 | async-start | bytes 1048576 | tf_op jit(solution)/shard_map/all_to_all | solution.py:116
  168.9 49.5 %copy-start.3 = (f32[216,216]{1,0:T(8,128)S(1)}, f32[216,216]{1,0:T(8,128)}, u32[]{:S(2)}) copy-start(f32[216,216]{1,0:T(8,128)} %param.7) | copy-start | bytes 559876
  211.5 13.4 %all-to-all-start.11 = ((f32[8,32,247]{2,1,0:T(8,128)}), f32[8,32,247]{2,1,0:T(8,128)S(1)}, u32[]{:S(2)}, u32[]{:S(2)}) async-start(f32[8,32,247]{2,1,0:T(8,128)} %broadcast_in_dim.14), calls=%async_computation.11 | async-start | bytes 524288 | tf_op jit(solution)/shard_map/all_to_all | solution.py:34
where the time goes:
time: 228 us; the launch traced here: 227 us
  blocking collectives  125 us (55%)
  waiting for transfers between devices  31.5 us (14%)
  matrix products  24.6 us (11%)
  local copies, waits for them, and re-layouts  22.6 us (10%)
  starting transfers between devices  15.8 us (7%)
  other arithmetic  6.28 us (3%)
    all_to_all x3, blocking collectives, copy_for_each(): lax.all_to_all(jnp.broadcast_to(array[None], (size, *array.shape)), axis,...  41.4 us
    all_to_all x1, blocking collectives, local(): lax.all_to_all(inputs, TENSOR, split_axis=0, concat_axis=1, tiled=True)  20.1 us
    all_to_all x1, waiting for transfers between devices, summed_rows(): lax.all_to_all(nearer.astype(jnp.bfloat16), far, split_axis=0, concat_axi...  20 us
    all_to_all x1, blocking collectives, sum_by_axis(): lax.all_to_all(nearer, far, split_axis=0, concat_axis=0, tiled=True)  17.7 us
    all_to_all x1, blocking collectives, local(): lax.all_to_all(clipped_grad.astype(jnp.bfloat16), TENSOR, split_axis=0, c...  15.5 us
    all_to_all x1, blocking collectives, local(): lax.all_to_all(clipped, TENSOR, split_axis=1, concat_axis=0, tiled=True)  15 us
    all_to_all x1, blocking collectives, sum_at_owner(): blocks = lax.all_to_all(split_up(array, dim, size), axis, 0, 0, tiled=True)  9.18 us
    dot_general x1, matrix products, local(): jnp.dot(clipped_back.reshape(tok_rows, -1), weight_rows, preferred_elemen...  8.08 us
  transfers between devices with their start and end apart: 3, of which 3 were waited for; matrix products, arithmetic and copies ran while one was open for 3% of the time, Pallas kernels for 0%

commit v1 on v0

v1 whole, which is shorter than its diff:
```python
import functools

import jax
import jax.numpy as jnp
from jax import lax
from jax.experimental import pallas as pl
from jax.experimental.pallas import tpu as pltpu
from jax.sharding import Mesh
from jax.sharding import PartitionSpec as P

CHIPS = ("chip_x", "chip_y")
TENSOR = (*CHIPS, "core")
F32, BF16 = jnp.float32, jnp.bfloat16
TN = (((0,), (0,)), ((), ()))
NT = (((1,), (1,)), ((), ()))
NN = (((1,), (0,)), ((), ()))

LANES, WIDE = 128, 256
TOK = 8


def call(kernel, outs, name, flops=0, moved=0, vmem=48, **kw):
    return pl.pallas_call(
        kernel,
        out_shape=outs,
        compiler_params=pltpu.CompilerParams(vmem_limit_bytes=vmem << 20),
        cost_estimate=pl.CostEstimate(flops=flops, bytes_accessed=moved, transcendentals=0),
        name=name,
        **kw,
    )


def shape(*lengths, dtype=BF16):
    return jax.ShapeDtypeStruct(lengths, dtype)


def halves(a):
    high = a.astype(BF16)
    return high, (a - high.astype(F32)).astype(BF16)


def dot(a, b, dims):
    return lax.dot_general(a, b, dims, preferred_element_type=F32)


def dot3(a, b, dims):
    (a_high, a_low), (b_high, b_low) = a, b
    return dot(a_high, b_high, dims) + (dot(a_high, b_low, dims) + dot(a_low, b_high, dims))


def of_token(ref, token, count):
    rows = pl.ds(token, count, stride=TOK)
    return jnp.concatenate([ref[0, rows, :], ref[1, rows, :]], axis=1)


def put_token(ref, token, value):
    rows = pl.ds(token, value.shape[0], stride=TOK)
    ref[0, rows, :] = value[:, :LANES]
    ref[1, rows, :] = value[:, LANES:]


def joined(ref):
    return jnp.concatenate([ref[0], ref[1]], axis=1)


def widened(a, rows, value=0.0):
    return jnp.pad(a, ((0, rows - a.shape[0]), (0, WIDE - a.shape[1])), constant_values=value)


def by_token_kernel(width, x_ref, o_ref):
    for j in range(o_ref.shape[2]):
        part = x_ref[j * width : (j + 1) * width, :].astype(F32)
        part = jnp.pad(part, ((0, WIDE - width), (0, 0)))
        turned = part.T.astype(BF16)
        half = turned.shape[0] // 2
        for core in range(2):
            o_ref[:, core, j] = turned[core * half : (core + 1) * half].reshape(-1, TOK, WIDE)


def forward_kernel(x_ref, left_ref, right_ref, scale_ref, clip_ref, slope_ref, mixed_ref, hold_ref):
    right_count = right_ref.shape[0]
    left_high, left_low = halves(widened(left_ref[...], WIDE))
    x = x_ref[...]
    mixed = dot(x, left_high, NN) + dot(x, left_low, NN)
    mixed_ref[0] = mixed[:, :LANES]
    mixed_ref[1] = mixed[:, LANES:]
    turned = halves(right_ref[...].T)
    scale = widened(scale_ref[...].T, right_count, 1.0)
    inverse = 1.0 / scale
    for t in range(TOK):
        rotated = dot3(turned, halves(of_token(mixed_ref, t, right_count)), NN)
        bounded = jnp.tanh(rotated * inverse)
        put_token(hold_ref, t, scale * bounded)
        put_token(slope_ref, t, 1.0 - bounded * bounded)
    clip_ref[...] = joined(hold_ref).astype(BF16)


def project_kernel(width, core_ref, clip_ref, own_ref, other_ref, o_ref):
    core = core_ref[0]
    chips = clip_ref.shape[0]
    each = own_ref.shape[0] // width
    total = None
    for ref, base in ((own_ref, core * each), (other_ref, (1 - core) * each)):
        for j in range(each):
            start = pl.multiple_of((base + j) * TOK, TOK)
            part = clip_ref[:, pl.ds(start, TOK), :].reshape(chips * TOK, WIDE)
            term = dot(part[:, :width], ref[j * width : (j + 1) * width, :], NN)
            total = term if total is None else total + term
    o_ref[...] = total.astype(BF16)


def residual_kernel(parts_ref, target_ref, o_ref):
    total = jnp.sum(parts_ref[...].astype(F32), axis=0)
    grad = (total - target_ref[...].astype(F32)).astype(BF16)
    o_ref[...] = jnp.broadcast_to(grad[None], o_ref.shape)


def back_project_kernel(core_ref, grad_ref, own_ref, other_ref, o_ref):
    step = pl.program_id(0)
    each = pl.num_programs(0) // 2
    core = core_ref[0]
    chips = o_ref.shape[0]

    def put(ref, index):
        part = dot(grad_ref[...], ref[...], NT)
        part = widened(part, part.shape[0]).astype(BF16)
        start = pl.multiple_of(index * TOK, TOK)
        o_ref[:, pl.ds(start, TOK), :] = part.reshape(chips, TOK, WIDE)

    @pl.when(step < each)
    def _():
        put(own_ref, core * each + step)

    @pl.when(step >= each)
    def _():
        put(other_ref, (1 - core) * each + step - each)


def backward_kernel(width, grad_ref, slope_ref, mixed_ref, x_ref, right_ref, o_ref, hold_ref, back_ref):
    right_count = right_ref.shape[0]
    owners = o_ref.shape[0]
    own_rows = x_ref.shape[0] // owners
    for side in range(2):
        lanes = slice(side * LANES, (side + 1) * LANES)
        hold_ref[side] = grad_ref[:, lanes].astype(F32) * slope_ref[side]
    right = halves(right_ref[...])
    grad_right = None
    for t in range(TOK):
        rotated_grad = halves(of_token(hold_ref, t, right_count))
        put_token(back_ref, t, dot3(right, rotated_grad, NN))
        term = dot3(halves(of_token(mixed_ref, t, right_count)), rotated_grad, NT)
        grad_right = term if grad_right is None else grad_right + term
    high, low = halves(joined(back_ref))
    x = x_ref[...]
    grad_left = dot(x, high, TN) + dot(x, low, TN)
    o_ref[:, :own_rows, :] = high.reshape(owners, own_rows, WIDE)
    o_ref[:, own_rows:, :] = jnp.zeros((owners, 2 * TOK, WIDE), BF16)
    left_count, right_rows = width // TOK, right_count // TOK
    o_ref[:left_count, own_rows : own_rows + TOK, :] = (
        grad_left[:width].reshape(left_count, TOK, WIDE).astype(BF16)
    )
    o_ref[:right_rows, own_rows + TOK :, :right_count] = grad_right.reshape(
        right_rows, TOK, right_count
    ).astype(BF16)


def input_grad_kernel(back_ref, left_ref, o_ref, factor_ref):
    chips, _, total, _ = back_ref.shape
    width = left_ref.shape[0]
    count = total // TOK - 2
    left_high, left_low = halves(widened(left_ref[...], width))
    half = chips * TOK
    for j in range(count):
        for core in range(2):
            part = back_ref[:, core, j * TOK : (j + 1) * TOK, :].reshape(half, WIDE)
            o_ref[j * width : (j + 1) * width, core * half : (core + 1) * half] = dot(
                left_high, part, NT
            ) + dot(left_low, part, NT)
    factors = back_ref[:, :, count * TOK :, :].astype(F32)
    factor_ref[...] = jnp.broadcast_to(jnp.sum(factors, axis=(0, 1))[None], factor_ref.shape)


def sum_and_copy_kernel(parts_ref, o_ref):
    o_ref[...] = jnp.broadcast_to(jnp.sum(parts_ref[...], axis=0)[None], o_ref.shape)


def unpack_kernel(parts_ref, left_ref, right_ref):
    width, count = left_ref.shape[0], right_ref.shape[0]
    left_ref[...] = parts_ref[: width // TOK, :TOK, :].reshape(width, WIDE)[:, :width]
    right_ref[...] = parts_ref[: count // TOK, TOK:, :count].reshape(count, count)


def exchange(array, axes):
    return lax.all_to_all(array, axes, split_axis=0, concat_axis=0, tiled=True)


def local(activations, left_factor, right_factor, clip_scale, weight_rows, target):
    tokens, hidden = activations.shape
    width, right_count = left_factor.shape[0], right_factor.shape[0]
    columns = weight_rows.shape[1]
    each = hidden // width
    chips = lax.axis_size(CHIPS)
    owners = 2 * chips
    half = tokens // 2
    rows = right_count * TOK
    core = lax.axis_index("core")
    core_operand = core.reshape(1)

    other_rows = lax.ppermute(weight_rows, "core", [(0, 1), (1, 0)])

    by_token = call(
        functools.partial(by_token_kernel, width),
        shape(chips, 2, each, TOK, WIDE), "by_token", 0, 4 * tokens * hidden
    )(activations.T)
    moved = exchange(by_token.reshape(owners, each * TOK, WIDE), TENSOR).reshape(rows, WIDE)

    lanes_apart = shape(2, rows, LANES, dtype=F32)
    hold = pltpu.VMEM((2, rows, LANES), F32)
    clipped, slope, mixed = call(
        forward_kernel,
        (shape(rows, WIDE), lanes_apart, lanes_apart),
        "forward",
        4 * rows * width * width + 6 * rows * width * right_count,
        12 * rows * width,
        scratch_shapes=[hold],
    )(moved, left_factor, right_factor, clip_scale.T)
    clipped_back = exchange(clipped.reshape(chips, 2 * each * TOK, WIDE), CHIPS)

    block = 1024
    smem = pl.BlockSpec(memory_space=pltpu.SMEM)
    partial_out = call(
        functools.partial(project_kernel, width),
        shape(half, columns),
        "project",
        4 * half * hidden * columns,
        4 * hidden * columns,
        grid=(columns // block,),
        in_specs=[
            smem,
            pl.BlockSpec((chips, 2 * each * TOK, WIDE), lambda i: (0, 0, 0)),
            pl.BlockSpec((hidden, block), lambda i: (0, i)),
            pl.BlockSpec((hidden, block), lambda i: (0, i)),
        ],
        out_specs=pl.BlockSpec((half, block), lambda i: (0, i)),
    )(core_operand, clipped_back, weight_rows, other_rows)
    arrived = exchange(partial_out.reshape(chips, TOK, columns), CHIPS)

    own = core * half + lax.axis_index(CHIPS) * TOK
    own_target = lax.dynamic_slice_in_dim(target, own, TOK, 0)
    grad_copies = call(
        residual_kernel, shape(chips, TOK, columns), "residual", 0, 4 * half * columns
    )(arrived, own_target)
    out_grad = exchange(grad_copies, CHIPS).reshape(half, columns)

    clipped_grad = call(
        back_project_kernel,
        shape(chips, 2 * each * TOK, WIDE),
        "back_project",
        4 * half * hidden * columns,
        4 * hidden * columns,
        grid=(2 * each,),
        in_specs=[
            smem,
            pl.BlockSpec((half, columns), lambda i: (0, 0)),
            pl.BlockSpec((width, columns), lambda i: (jnp.minimum(i, each - 1), 0)),
            pl.BlockSpec((width, columns), lambda i: (jnp.maximum(i - each, 0), 0)),
        ],
        out_specs=pl.BlockSpec((chips, 2 * each * TOK, WIDE), lambda i: (0, 0, 0)),
    )(core_operand, out_grad, weight_rows, other_rows)
    grad_owned = exchange(clipped_grad, CHIPS).reshape(rows, WIDE)

    per_owner = (each + 2) * TOK
    packed = call(
        functools.partial(backward_kernel, width),
        shape(owners, per_owner, WIDE),
        "backward",
        4 * rows * width * width + 12 * rows * width * right_count,
        14 * rows * width,
        scratch_shapes=[hold, hold],
    )(grad_owned, slope, mixed, moved, right_factor)
    back = exchange(packed, TENSOR).reshape(chips, 2, per_owner, WIDE)

    groups = lax.axis_size("dp")
    input_grad, factor_copies = call(
        input_grad_kernel,
        (shape(hidden, tokens, dtype=F32), shape(groups, 2 * TOK, WIDE, dtype=F32)),
        "input_grad",
        4 * tokens * hidden * width,
        6 * tokens * hidden,
    )(back, left_factor)
    factor_parts = exchange(factor_copies, "dp")
    factor_sums = call(
        sum_and_copy_kernel, shape(owners, 2 * TOK, WIDE, dtype=F32), "sum_and_copy", 0, 1 << 20
    )(factor_parts)
    gathered = exchange(factor_sums, TENSOR)
    left_sum, right_sum = call(
        unpack_kernel,
        (shape(width, width, dtype=F32), shape(right_count, right_count, dtype=F32)),
        "unpack",
        0,
        1 << 19,
    )(gathered)
    return left_sum, right_sum, input_grad.T


def solution(mesh):
    torus = Mesh(mesh.devices.reshape(mesh.shape["dp"], 4, 4, 2), ("dp", *TENSOR))
    placed = (P("dp", TENSOR), P(), P(), P(), P(TENSOR, None), P("dp", None))
    return jax.shard_map(
        local, mesh=torus, in_specs=placed, out_specs=(P(), P(), P("dp", TENSOR)), check_vma=False
    )
```

time: 228 us -> 186 us (0.82)
  Pallas kernels: 0 us -> 28.1 us
  matrix products: 24.6 us -> 0 us
  blocking collectives: 125 us -> 106 us
  local copies, waits for them, and re-layouts: 22.6 us -> 7.62 us
  other arithmetic: 6.28 us -> 0 us
  starting transfers between devices: 15.8 us -> 12 us
    pallas_call x0 -> x9, Pallas kernels: none -> 28.1 us  [the longest x1 12 us: local(): call(back_project_kernel, shape(chips, 2 * each * TOK, WIDE), 'back_proje...]
    dot_general x8 -> x0, matrix products: 24.6 us -> none  [the longest x1 8.08 us: local(): jnp.dot(clipped_back.reshape(tok_rows, -1), weight_rows, preferred_elemen...]
    all_to_all x9 -> x6, blocking collectives: 125 us -> 106 us  [exchange(): return lax.all_to_all(array, axes, split_axis=0, concat_axis=0, tiled=True)]
    convert_element_type x6 -> x0, local copies, waits for them, and re-layouts: 12 us -> none  [the longest x1 4.39 us: local(): partial_out.astype(jnp.bfloat16)]
    all_to_all x3 -> x2, starting transfers between devices: 15.8 us -> 8.64 us  [exchange(): return lax.all_to_all(array, axes, split_axis=0, concat_axis=0, tiled=True)]
    unnamed x20 -> x26, local copies, waits for them, and re-layouts: 1.06 us -> 7.61 us
    reduce_sum x4 -> x0, other arithmetic: 5.25 us -> none  [the longest x1 3.67 us: summed_on_arrival(): return jnp.sum(blocks.astype(jnp.float32), axis=0)]
    reshape x5 -> x0, local copies, waits for them, and re-layouts: 4.63 us -> none  [the longest x2 1.73 us: packed_total(): done.append(total[at:at + a.size].reshape(a.shape))]
  transfers between devices with their start and end apart: 3 -> 3, of which waited for: 3 -> 2; matrix products, arithmetic and copies ran while one was open for 3% -> 0% of each run, Pallas kernels for 0% -> 1%
where the time goes in v1:
time: 186 us; the launch traced here: 185 us
  blocking collectives  106 us (57%)
  waiting for transfers between devices  29.9 us (16%)
  Pallas kernels  28.1 us (15%)
  starting transfers between devices  12 us (6%)
  local copies, waits for them, and re-layouts  7.62 us (4%)
    all_to_all x6, blocking collectives, exchange(): return lax.all_to_all(array, axes, split_axis=0, concat_axis=0, tiled=True)  106 us
    all_to_all x2, waiting for transfers between devices, exchange(): return lax.all_to_all(array, axes, split_axis=0, concat_axis=0, tiled=True)  29.9 us
    pallas_call x1, Pallas kernels, local(): call(back_project_kernel, shape(chips, 2 * each * TOK, WIDE), 'back_proje...  12 us
    all_to_all x2, starting transfers between devices, exchange(): return lax.all_to_all(array, axes, split_axis=0, concat_axis=0, tiled=True)  8.64 us
    pallas_call x1, Pallas kernels, local(): call(functools.partial(project_kernel, width), shape(half, columns), 'pro...  8.61 us
    unnamed x26, local copies, waits for them, and re-layouts  7.61 us
  transfers between devices with their start and end apart: 3, of which 2 were waited for; matrix products, arithmetic and copies ran while one was open for 0% of the time, Pallas kernels for 1%

profile of v1, /device:TPU:1, one launch (start us, length us, event | category | flops | bytes accessed | tf_op | source)
XLA Modules:
  0.0 184.8 jit_solution(479498678833181178)
XLA Ops:
  0.6 0.0 copy-start
  0.6 3.3 %collective-permute-start = (bf16[864,5120]{1,0:T(8,128)(2,1)}, bf16[864,5120]{1,0:T(8,128)(2,1)}, u32[]{:S(2)}, u32[]{:S(2)}) collective-permute-start(bf16[864,5120]{1,0:T(8,128)(2,1)} %own_ref.3), channel_id=1, source_target_pairs={{0,1},{1,0},{2,3},{3,2},{4,5},{5,4},{6,7},{7,6},{8,9},{9,8},{10,11... | collective-permute-start | bytes 26542088 | tf_op jit(solution)/shard_map/ppermute | solution.py:209
  4.0 1.0 copy-done.7
  5.0 0.2 by_token.1
  5.2 17.0 %all_to_all.40 = bf16[32,32,256]{2,1,0:T(8,128)(2,1)S(1)} all-to-all(bf16[32,32,256]{2,1,0:T(8,128)(2,1)S(1)} %bitcast.17), channel_id=1, replica_groups=mesh['dp'=8,'chip_x'=4,'chip_y'=4,'core'=2] {'chip_x','chip_y','core'}, dimensions={0} | all-to-all | bytes 1048576 | tf_op jit(solution)/shard_map/all_to_all | solution.py:194
  22.2 0.9 copy-done.8
  23.1 0.8 copy-done.10
  23.9 0.9 copy-done.12
  24.8 1.9 %forward.1 = (bf16[1024,256]{1,0:T(8,128)(2,1)S(1)}, f32[2,1024,128]{2,1,0:T(8,128)S(1)}, f32[2,1024,128]{2,1,0:T(8,128)S(1)}) custom-call(bf16[1024,256]{1,0:T(8,128)(2,1)S(1)} %bitcast.14, f32[216,216]{1,0:T(8,128)S(1)} %copy-done.8, f32[128,128]{1,0:T(8,128)S(1)} %copy-done.10, f32[216,128]{1,0:T(8,128)S(1)} %bitcast.20), custom_call_target="tpu_custom_call" | custom-call | flops 360972288 | bytes 2654208 | tf_op jit(solution)/shard_map/forward/pallas_call | solution.py:219
  26.7 1.0 copy-done.2
  27.7 1.0 copy-done.4
  28.7 0.8 copy-done.6
  29.5 4.2 %all-to-all-start.1 = ((bf16[16,64,256]{2,1,0:T(8,128)(2,1)}), bf16[16,64,256]{2,1,0:T(8,128)(2,1)}, u32[]{:S(2)}, u32[]{:S(2)}) async-start(bf16[16,64,256]{2,1,0:T(8,128)(2,1)} %bitcast.18), calls=%async_computation.1 | async-start | bytes 1048576 | tf_op jit(solution)/shard_map/all_to_all | solution.py:194
  33.8 11.7 %all-to-all-done.1.clip_ref = bf16[16,64,256]{2,1,0:T(8,128)(2,1)} async-done(((bf16[16,64,256]{2,1,0:T(8,128)(2,1)}), bf16[16,64,256]{2,1,0:T(8,128)(2,1)}, u32[]{:S(2)}, u32[]{:S(2)}) %all-to-all-start.1) | async-done | bytes 524320 | tf_op jit(solution)/shard_map/all_to_all | solution.py:194
  45.5 0.0 collective-permute-done.other_ref
  45.5 8.6 %project.1 = bf16[128,5120]{1,0:T(8,128)(2,1)S(1)} custom-call(s32[1]{0:T(128)} %bitcast.core_ref, bf16[16,64,256]{2,1,0:T(8,128)(2,1)} %all-to-all-done.1.clip_ref, bf16[864,5120]{1,0:T(8,128)(2,1)} %own_ref.3, bf16[864,5120]{1,0:T(8,128)(2,1)} %collective-permute-done.other_ref), custom_call_target="tpu_custom_call" | custom-call | flops 2264924160 | bytes 17694720 | tf_op jit(solution)/shard_map/project/pallas_call | solution.py:231
  54.1 1.1 copy-done.1
  55.2 4.4 %all-to-all-start.2 = ((bf16[16,8,5120]{2,1,0:T(8,128)(2,1)}), bf16[16,8,5120]{2,1,0:T(8,128)(2,1)}, u32[]{:S(2)}, u32[]{:S(2)}) async-start(bf16[16,8,5120]{2,1,0:T(8,128)(2,1)} %bitcast.11), calls=%async_computation.2 | async-start | bytes 2621440 | tf_op jit(solution)/shard_map/all_to_all | solution.py:194
  59.6 0.0 copy-done
  59.6 18.2 %all-to-all-done.2.parts_ref = bf16[16,8,5120]{2,1,0:T(8,128)(2,1)} async-done(((bf16[16,8,5120]{2,1,0:T(8,128)(2,1)}), bf16[16,8,5120]{2,1,0:T(8,128)(2,1)}, u32[]{:S(2)}, u32[]{:S(2)}) %all-to-all-start.2) | async-done | bytes 1310752 | tf_op jit(solution)/shard_map/all_to_all | solution.py:194
  77.9 1.5 residual.1
  79.4 22.1 %all_to_all.41 = bf16[16,8,5120]{2,1,0:T(8,128)(2,1)S(1)} all-to-all(bf16[16,8,5120]{2,1,0:T(8,128)(2,1)S(1)} %residual.1), channel_id=1, replica_groups=mesh['dp'=8,'chip_x'=4,'chip_y'=4,'core'=2] {'chip_x','chip_y'}, dimensions={0} | all-to-all | bytes 2621440 | tf_op jit(solution)/shard_map/all_to_all | solution.py:194
  101.5 12.0 %back_project.1 = bf16[16,64,256]{2,1,0:T(8,128)(2,1)S(1)} custom-call(s32[1]{0:T(128)} %bitcast.core_ref, bf16[128,5120]{1,0:T(8,128)(2,1)S(1)} %bitcast.12, bf16[864,5120]{1,0:T(8,128)(2,1)} %own_ref.3, bf16[864,5120]{1,0:T(8,128)(2,1)} %collective-permute-done.other_ref), custom_call_target="tpu_custom_call" | custom-call | flops 2264924160 | bytes 17694720 | tf_op jit(solution)/shard_map/back_project/pallas_call | solution.py:255
  113.5 12.2 %all_to_all.42 = bf16[16,64,256]{2,1,0:T(8,128)(2,1)S(1)} all-to-all(bf16[16,64,256]{2,1,0:T(8,128)(2,1)S(1)} %back_project.1), channel_id=1, replica_groups=mesh['dp'=8,'chip_x'=4,'chip_y'=4,'core'=2] {'chip_x','chip_y'}, dimensions={0} | all-to-all | bytes 1048576 | tf_op jit(solution)/shard_map/all_to_all | solution.py:194
  125.8 0.0 copy-start.9
  125.8 1.6 backward.1
  127.4 22.2 %all_to_all.43 = bf16[32,48,256]{2,1,0:T(8,128)(2,1)S(1)} all-to-all(bf16[32,48,256]{2,1,0:T(8,128)(2,1)S(1)} %backward.1), channel_id=1, replica_groups=mesh['dp'=8,'chip_x'=4,'chip_y'=4,'core'=2] {'chip_x','chip_y','core'}, dimensions={0} | all-to-all | bytes 1572864 | tf_op jit(solution)/shard_map/all_to_all | solution.py:194
  149.5 1.6 input_grad.1
  151.1 16.6 %all_to_all.44.parts_ref = f32[8,16,256]{2,1,0:T(8,128)S(1)} all-to-all(f32[8,16,256]{2,1,0:T(8,128)S(1)} %get-tuple-element.13), channel_id=1, replica_groups=mesh['dp'=8,'chip_x'=4,'chip_y'=4,'core'=2] {'dp'}, dimensions={0} | all-to-all | bytes 262144 | tf_op jit(solution)/shard_map/all_to_all | solution.py:194
  167.7 0.1 sum_and_copy.1
  167.8 16.3 %all_to_all.45.parts_ref = f32[32,16,256]{2,1,0:T(8,128)S(1)} all-to-all(f32[32,16,256]{2,1,0:T(8,128)S(1)} %sum_and_copy.1), channel_id=1, replica_groups=mesh['dp'=8,'chip_x'=4,'chip_y'=4,'core'=2] {'chip_x','chip_y','core'}, dimensions={0} | all-to-all | bytes 1048576 | tf_op jit(solution)/shard_map/all_to_all | solution.py:194
  184.1 0.7 unpack.1
  (16 shorter events, 0.0 us)
Async XLA Ops:
  0.6 59.0 %copy-start = (bf16[256,5120]{1,0:T(8,128)(2,1)S(1)}, bf16[256,5120]{1,0:T(8,128)(2,1)}, u32[]{:S(2)}) copy-start(bf16[256,5120]{1,0:T(8,128)(2,1)} %param.11) | copy-start | bytes 7864324
  0.6 44.8 %collective-permute-start = (bf16[864,5120]{1,0:T(8,128)(2,1)}, bf16[864,5120]{1,0:T(8,128)(2,1)}, u32[]{:S(2)}, u32[]{:S(2)}) collective-permute-start(bf16[864,5120]{1,0:T(8,128)(2,1)} %own_ref.3), channel_id=1, source_target_pairs={{0,1},{1,0},{2,3},{3,2},{4,5},{5,4},{6,7},{7,6},{8,9},{9,8},{10,11... | collective-permute-start | bytes 26542088 | tf_op jit(solution)/shard_map/ppermute | solution.py:209
  4.0 1.0 copy-start.7
  22.1 0.9 copy-start.8
  23.1 0.8 copy-start.10
  23.9 0.9 copy-start.12
  26.7 1.0 copy-start.2
  27.7 1.0 copy-start.4
  28.7 0.8 copy-start.6
  29.5 15.9 %all-to-all-start.1 = ((bf16[16,64,256]{2,1,0:T(8,128)(2,1)}), bf16[16,64,256]{2,1,0:T(8,128)(2,1)}, u32[]{:S(2)}, u32[]{:S(2)}) async-start(bf16[16,64,256]{2,1,0:T(8,128)(2,1)} %bitcast.18), calls=%async_computation.1 | async-start | bytes 1048576 | tf_op jit(solution)/shard_map/all_to_all | solution.py:194
  54.1 1.1 copy-start.1
  55.2 22.7 %all-to-all-start.2 = ((bf16[16,8,5120]{2,1,0:T(8,128)(2,1)}), bf16[16,8,5120]{2,1,0:T(8,128)(2,1)}, u32[]{:S(2)}, u32[]{:S(2)}) async-start(bf16[16,8,5120]{2,1,0:T(8,128)(2,1)} %bitcast.11), calls=%async_computation.2 | async-start | bytes 2621440 | tf_op jit(solution)/shard_map/all_to_all | solution.py:194
  101.5 24.3 %copy-start.3 = (f32[2,1024,128]{2,1,0:T(8,128)S(1)}, f32[2,1024,128]{2,1,0:T(8,128)}, u32[]{:S(2)}) copy-start(f32[2,1024,128]{2,1,0:T(8,128)} %copy-done.2) | copy-start | bytes 3145732
  101.5 24.3 %copy-start.5 = (f32[2,1024,128]{2,1,0:T(8,128)S(1)}, f32[2,1024,128]{2,1,0:T(8,128)}, u32[]{:S(2)}) copy-start(f32[2,1024,128]{2,1,0:T(8,128)} %copy-done.4) | copy-start | bytes 3145732
  101.5 24.3 %copy-start.11 = (f32[128,128]{1,0:T(8,128)S(1)}, f32[128,128]{1,0:T(8,128)}, u32[]{:S(2)}) copy-start(f32[128,128]{1,0:T(8,128)} %right_ref.3) | copy-start | bytes 196612
  125.8 23.8 %copy-start.9 = (f32[216,216]{1,0:T(8,128)S(1)}, f32[216,216]{1,0:T(8,128)}, u32[]{:S(2)}) copy-start(f32[216,216]{1,0:T(8,128)} %left_ref.3) | copy-start | bytes 559876

commit v2 on v1

--- a/solution.py
+++ b/solution.py
@@ -11,6 +11,7 @@
 CHIPS = ("chip_x", "chip_y")
 TENSOR = (*CHIPS, "core")
 F32, BF16 = jnp.float32, jnp.bfloat16
+HBM = pltpu.MemorySpace.HBM
 TN = (((0,), (0,)), ((), ()))
 NT = (((1,), (1,)), ((), ()))
 NN = (((1,), (0,)), ((), ()))
@@ -19,7 +20,7 @@
 TOK = 8
 
 
-def call(kernel, outs, name, flops=0, moved=0, vmem=48, **kw):
+def call(kernel, outs, name, flops=0, moved=0, vmem=16, **kw):
     return pl.pallas_call(
         kernel,
         out_shape=outs,
@@ -67,26 +68,47 @@
     return jnp.pad(a, ((0, rows - a.shape[0]), (0, WIDE - a.shape[1])), constant_values=value)
 
 
-def by_token_kernel(width, x_ref, o_ref):
-    for j in range(o_ref.shape[2]):
-        part = x_ref[j * width : (j + 1) * width, :].astype(F32)
+def first_kernel(width, *refs):
+    *sources, o_ref, left_ref, right_ref, scale_ref = refs[:8]
+    *buffers, sems = refs[8:]
+    x_hbm, x_buf = sources[0], buffers[0]
+    count = x_hbm.shape[0] // width
+    tall = 2 * width
+    cuts = [pl.ds(i * tall, tall) for i in range(count // 2)]
+    pairs = [(x_hbm.at[cut], x_buf.at[cut]) for cut in cuts] + list(zip(sources[1:], buffers[1:]))
+    copies = [
+        pltpu.make_async_copy(src, dst, sems.at[i]) for i, (src, dst) in enumerate(pairs)
+    ]
+    for copy in copies:
+        copy.start()
+    for j in range(count):
+        if j % 2 == 0:
+            copies[j // 2].wait()
+        part = x_buf[j * width : (j + 1) * width, :].astype(F32)
         part = jnp.pad(part, ((0, WIDE - width), (0, 0)))
         turned = part.T.astype(BF16)
         half = turned.shape[0] // 2
         for core in range(2):
             o_ref[:, core, j] = turned[core * half : (core + 1) * half].reshape(-1, TOK, WIDE)
+    for copy in copies[count // 2 :]:
+        copy.wait()
+    _, left_buf, right_buf, scale_buf = buffers
+    left_ref[0], left_ref[1] = halves(widened(left_buf[...], WIDE))
+    right_ref[0], right_ref[1] = halves(right_buf[...])
+    right_ref[2], right_ref[3] = halves(right_buf[...].T)
+    scale = widened(scale_buf[...].T, right_buf.shape[0], 1.0)
+    scale_ref[0] = scale
+    scale_ref[1] = 1.0 / scale
 
 
 def forward_kernel(x_ref, left_ref, right_ref, scale_ref, clip_ref, slope_ref, mixed_ref, hold_ref):
-    right_count = right_ref.shape[0]
-    left_high, left_low = halves(widened(left_ref[...], WIDE))
+    right_count = right_ref.shape[1]
     x = x_ref[...]
-    mixed = dot(x, left_high, NN) + dot(x, left_low, NN)
+    mixed = dot(x, left_ref[0], NN) + dot(x, left_ref[1], NN)
     mixed_ref[0] = mixed[:, :LANES]
     mixed_ref[1] = mixed[:, LANES:]
-    turned = halves(right_ref[...].T)
-    scale = widened(scale_ref[...].T, right_count, 1.0)
-    inverse = 1.0 / scale
+    turned = right_ref[2], right_ref[3]
+    scale, inverse = scale_ref[0], scale_ref[1]
     for t in range(TOK):
         rotated = dot3(turned, halves(of_token(mixed_ref, t, right_count)), NN)
         bounded = jnp.tanh(rotated * inverse)
@@ -95,8 +117,8 @@
     clip_ref[...] = joined(hold_ref).astype(BF16)
 
 
-def project_kernel(width, core_ref, clip_ref, own_ref, other_ref, o_ref):
-    core = core_ref[0]
+def project_kernel(width, place_ref, clip_ref, own_ref, other_ref, o_ref):
+    core = place_ref[0]
     chips = clip_ref.shape[0]
     each = own_ref.shape[0] // width
     total = None
@@ -109,16 +131,23 @@
     o_ref[...] = total.astype(BF16)
 
 
-def residual_kernel(parts_ref, target_ref, o_ref):
+def residual_kernel(place_ref, parts_ref, target_hbm, o_ref, rows_ref, sem):
+    pair = rows_ref.shape[0]
+    start = pl.multiple_of(place_ref[1] * pair, pair)
+    copy = pltpu.make_async_copy(target_hbm.at[pl.ds(start, pair)], rows_ref, sem)
+    copy.start()
     total = jnp.sum(parts_ref[...].astype(F32), axis=0)
-    grad = (total - target_ref[...].astype(F32)).astype(BF16)
+    copy.wait()
+    rows = rows_ref[...].astype(F32)
+    own = jnp.where(place_ref[2] == 1, rows[TOK:], rows[:TOK])
+    grad = (total - own).astype(BF16)
     o_ref[...] = jnp.broadcast_to(grad[None], o_ref.shape)
 
 
-def back_project_kernel(core_ref, grad_ref, own_ref, other_ref, o_ref):
+def back_project_kernel(place_ref, grad_ref, own_ref, other_ref, o_ref):
     step = pl.program_id(0)
     each = pl.num_programs(0) // 2
-    core = core_ref[0]
+    core = place_ref[0]
     chips = o_ref.shape[0]
 
     def put(ref, index):
@@ -136,14 +165,31 @@
         put(other_ref, (1 - core) * each + step - each)
 
 
+def packed_factors(width, grad_left, grad_right):
+    low = WIDE - width
+    rest = widened(grad_right[2 * low :], grad_right.shape[0] - 2 * low)
+    height = rest.shape[0]
+    lane = lax.broadcasted_iota(jnp.int32, (height, WIDE), 1)
+    pieces = []
+    for m in range(width // height):
+        top = grad_left[m * height : (m + 1) * height]
+        if m * low < grad_right.shape[1]:
+            moved = pltpu.roll(rest, width - m * low, axis=1)
+            top = jnp.where(lane < width, top, moved)
+        pieces.append(top)
+    pieces.append(grad_left[width // height * height : width])
+    bottom = jnp.concatenate([grad_right[:low], grad_right[low : 2 * low]], axis=1)
+    return jnp.concatenate([*pieces, bottom], axis=0)
+
+
 def backward_kernel(width, grad_ref, slope_ref, mixed_ref, x_ref, right_ref, o_ref, hold_ref, back_ref):
-    right_count = right_ref.shape[0]
+    right_count = right_ref.shape[1]
     owners = o_ref.shape[0]
     own_rows = x_ref.shape[0] // owners
     for side in range(2):
         lanes = slice(side * LANES, (side + 1) * LANES)
         hold_ref[side] = grad_ref[:, lanes].astype(F32) * slope_ref[side]
-    right = halves(right_ref[...])
+    right = right_ref[0], right_ref[1]
     grad_right = None
     for t in range(TOK):
         rotated_grad = halves(of_token(hold_ref, t, right_count))
@@ -154,22 +200,15 @@
     x = x_ref[...]
     grad_left = dot(x, high, TN) + dot(x, low, TN)
     o_ref[:, :own_rows, :] = high.reshape(owners, own_rows, WIDE)
-    o_ref[:, own_rows:, :] = jnp.zeros((owners, 2 * TOK, WIDE), BF16)
-    left_count, right_rows = width // TOK, right_count // TOK
-    o_ref[:left_count, own_rows : own_rows + TOK, :] = (
-        grad_left[:width].reshape(left_count, TOK, WIDE).astype(BF16)
-    )
-    o_ref[:right_rows, own_rows + TOK :, :right_count] = grad_right.reshape(
-        right_rows, TOK, right_count
-    ).astype(BF16)
-
-
-def input_grad_kernel(back_ref, left_ref, o_ref, factor_ref):
+    packed = packed_factors(width, grad_left, grad_right)
+    o_ref[:, own_rows:, :] = packed.reshape(owners, TOK, WIDE).astype(BF16)
+
+
+def input_grad_kernel(width, back_ref, left_ref, o_ref, factor_ref):
     chips, _, total, _ = back_ref.shape
-    width = left_ref.shape[0]
-    count = total // TOK - 2
-    left_high, left_low = halves(widened(left_ref[...], width))
+    count = total // TOK - 1
     half = chips * TOK
+    left_high, left_low = left_ref[0, :width], left_ref[1, :width]
     for j in range(count):
         for core in range(2):
             part = back_ref[:, core, j * TOK : (j + 1) * TOK, :].reshape(half, WIDE)
@@ -186,8 +225,22 @@
 
 def unpack_kernel(parts_ref, left_ref, right_ref):
     width, count = left_ref.shape[0], right_ref.shape[0]
-    left_ref[...] = parts_ref[: width // TOK, :TOK, :].reshape(width, WIDE)[:, :width]
-    right_ref[...] = parts_ref[: count // TOK, TOK:, :count].reshape(count, count)
+    packed = parts_ref[...].reshape(WIDE, WIDE)
+    left_ref[...] = packed[:width, :width]
+    low = WIDE - width
+    right_ref[:low, :] = packed[width:, :count]
+    right_ref[low : 2 * low, :] = packed[width:, count:]
+    height = count - 2 * low
+    lane = lax.broadcasted_iota(jnp.int32, (height, WIDE), 1)
+    rest = jnp.zeros((height, WIDE), F32)
+    for m in range(-(-count // low)):
+        back = pltpu.roll(packed[m * height : (m + 1) * height], WIDE - width + m * low, axis=1)
+        rest = jnp.where((lane >= m * low) & (lane < (m + 1) * low), back, rest)
+    right_ref[2 * low :, :] = rest[:, :count]
+
+
+def in_hbm(array):
+    return pltpu.with_memory_space_constraint(array, HBM)
 
 
 def exchange(array, axes):
@@ -204,14 +257,33 @@
     half = tokens // 2
     rows = right_count * TOK
     core = lax.axis_index("core")
-    core_operand = core.reshape(1)
+    slot = core * chips + lax.axis_index(CHIPS)
+    place = jnp.stack([core, slot // 2, slot % 2])
 
     other_rows = lax.ppermute(weight_rows, "core", [(0, 1), (1, 0)])
 
-    by_token = call(
-        functools.partial(by_token_kernel, width),
-        shape(chips, 2, each, TOK, WIDE), "by_token", 0, 4 * tokens * hidden
-    )(activations.T)
+    turned_x, turned_scale = activations.T, clip_scale.T
+    by_token, left_parts, right_parts, scales = call(
+        functools.partial(first_kernel, width),
+        (
+            shape(chips, 2, each, TOK, WIDE),
+            shape(2, WIDE, WIDE),
+            shape(4, right_count, right_count),
+            shape(2, right_count, WIDE, dtype=F32),
+        ),
+        "first",
+        0,
+        4 * tokens * hidden,
+        in_specs=[pl.BlockSpec(memory_space=HBM)] * 4,
+        scratch_shapes=[
+            pltpu.VMEM(turned_x.shape, BF16),
+            pltpu.VMEM(left_factor.shape, F32),
+            pltpu.VMEM(right_factor.shape, F32),
+            pltpu.VMEM(turned_scale.shape, F32),
+            pltpu.SemaphoreType.DMA((each // 2 + 3,)),
+        ],
+    )(*map(in_hbm, (turned_x, left_factor, right_factor, turned_scale)))
+    by_token, place = lax.optimization_barrier((by_token, place))
     moved = exchange(by_token.reshape(owners, each * TOK, WIDE), TENSOR).reshape(rows, WIDE)
 
     lanes_apart = shape(2, rows, LANES, dtype=F32)
@@ -223,7 +295,7 @@
         4 * rows * width * width + 6 * rows * width * right_count,
         12 * rows * width,
         scratch_shapes=[hold],
-    )(moved, left_factor, right_factor, clip_scale.T)
+    )(moved, left_parts, right_parts, scales)
     clipped_back = exchange(clipped.reshape(chips, 2 * each * TOK, WIDE), CHIPS)
 
     block = 1024
@@ -242,14 +314,18 @@
             pl.BlockSpec((hidden, block), lambda i: (0, i)),
         ],
         out_specs=pl.BlockSpec((half, block), lambda i: (0, i)),
-    )(core_operand, clipped_back, weight_rows, other_rows)
+    )(place, clipped_back, in_hbm(weight_rows), in_hbm(other_rows))
     arrived = exchange(partial_out.reshape(chips, TOK, columns), CHIPS)
 
-    own = core * half + lax.axis_index(CHIPS) * TOK
-    own_target = lax.dynamic_slice_in_dim(target, own, TOK, 0)
     grad_copies = call(
-        residual_kernel, shape(chips, TOK, columns), "residual", 0, 4 * half * columns
-    )(arrived, own_target)
+        residual_kernel,
+        shape(chips, TOK, columns),
+        "residual",
+        0,
+        4 * half * columns,
+        in_specs=[smem, pl.BlockSpec(), pl.BlockSpec(memory_space=HBM)],
+        scratch_shapes=[pltpu.VMEM((2 * TOK, columns), BF16), pltpu.SemaphoreType.DMA(())],
+    )(place, arrived, in_hbm(target))
     out_grad = exchange(grad_copies, CHIPS).reshape(half, columns)
 
     clipped_grad = call(
@@ -266,10 +342,10 @@
             pl.BlockSpec((width, columns), lambda i: (jnp.maximum(i - each, 0), 0)),
         ],
         out_specs=pl.BlockSpec((chips, 2 * each * TOK, WIDE), lambda i: (0, 0, 0)),
-    )(core_operand, out_grad, weight_rows, other_rows)
+    )(place, out_grad, weight_rows, other_rows)
     grad_owned = exchange(clipped_grad, CHIPS).reshape(rows, WIDE)
 
-    per_owner = (each + 2) * TOK
+    per_owner = (each + 1) * TOK
     packed = call(
         functools.partial(backward_kernel, width),
         shape(owners, per_owner, WIDE),
@@ -277,20 +353,20 @@
         4 * rows * width * width + 12 * rows * width * right_count,
         14 * rows * width,
         scratch_shapes=[hold, hold],
-    )(grad_owned, slope, mixed, moved, right_factor)
+    )(grad_owned, slope, mixed, moved, right_parts)
     back = exchange(packed, TENSOR).reshape(chips, 2, per_owner, WIDE)
 
     groups = lax.axis_size("dp")
     input_grad, factor_copies = call(
-        input_grad_kernel,
-        (shape(hidden, tokens, dtype=F32), shape(groups, 2 * TOK, WIDE, dtype=F32)),
+        functools.partial(input_grad_kernel, width),
+        (shape(hidden, tokens, dtype=F32), shape(groups, TOK, WIDE, dtype=F32)),
         "input_grad",
         4 * tokens * hidden * width,
         6 * tokens * hidden,
-    )(back, left_factor)
+    )(back, left_parts)
     factor_parts = exchange(factor_copies, "dp")
     factor_sums = call(
-        sum_and_copy_kernel, shape(owners, 2 * TOK, WIDE, dtype=F32), "sum_and_copy", 0, 1 << 20
+        sum_and_copy_kernel, shape(owners, TOK, WIDE, dtype=F32), "sum_and_copy", 0, 1 << 20
     )(factor_parts)
     gathered = exchange(factor_sums, TENSOR)
     left_sum, right_sum = call(

time: 186 us -> 169 us (0.909)
  waiting for transfers between devices: 29.9 us -> 0.01 us
  blocking collectives: 106 us -> 135 us
  starting transfers between devices: 12 us -> 3.33 us
  local copies, waits for them, and re-layouts: 7.62 us -> 0.02 us
    all_to_all x2 -> x0, waiting for transfers between devices: 29.9 us -> none  [exchange(): return lax.all_to_all(array, axes, split_axis=0, concat_axis=0, tiled=True)]
    all_to_all x6 -> x8, blocking collectives: 106 us -> 135 us  [exchange(): return lax.all_to_all(array, axes, split_axis=0, concat_axis=0, tiled=True)]
    all_to_all x2 -> x0, starting transfers between devices: 8.64 us -> none  [exchange(): return lax.all_to_all(array, axes, split_axis=0, concat_axis=0, tiled=True)]
    unnamed x26 -> x6, local copies, waits for them, and re-layouts: 7.61 us -> 0.02 us
  transfers between devices with their start and end apart: 3 -> 1, of which waited for: 2 -> 0; matrix products, arithmetic and copies ran while one was open for 0% -> 0% of each run, Pallas kernels for 1% -> 2%
where the time goes in v2:
time: 169 us; the launch traced here: 168 us
  blocking collectives  135 us (80%)
  Pallas kernels  29.4 us (17%)
  starting transfers between devices  3.33 us (2%)
    all_to_all x8, blocking collectives, exchange(): return lax.all_to_all(array, axes, split_axis=0, concat_axis=0, tiled=True)  135 us
    pallas_call x1, Pallas kernels, local(): call(back_project_kernel, shape(chips, 2 * each * TOK, WIDE), 'back_proje...  10.4 us
    pallas_call x1, Pallas kernels, local(): call(functools.partial(project_kernel, width), shape(half, columns), 'pro...  10.2 us
  transfers between devices with their start and end apart: 1, of which 0 were waited for; matrix products, arithmetic and copies ran while one was open for 0% of the time, Pallas kernels for 2%

profile of v2, /device:TPU:1, one launch (start us, length us, event | category | flops | bytes accessed | tf_op | source)
XLA Modules:
  0.0 168.2 jit_solution(6593766354881750450)
XLA Ops:
  0.6 3.3 %collective-permute-start = (bf16[864,5120]{1,0:T(8,128)(2,1)}, bf16[864,5120]{1,0:T(8,128)(2,1)}, u32[]{:S(2)}, u32[]{:S(2)}) collective-permute-start(bf16[864,5120]{1,0:T(8,128)(2,1)} %own_ref.3), channel_id=1, source_target_pairs={{0,1},{1,0},{2,3},{3,2},{4,5},{5,4},{6,7},{7,6},{8,9},{9,8},{10,11... | collective-permute-start | bytes 26542088 | tf_op jit(solution)/shard_map/ppermute | solution.py:263
  4.0 1.4 first.1
  5.4 0.1 pad_add_fusion.place_ref
  5.5 16.9 %all_to_all.40 = bf16[32,32,256]{2,1,0:T(8,128)(2,1)S(1)} all-to-all(bf16[32,32,256]{2,1,0:T(8,128)(2,1)S(1)} %bitcast.21), channel_id=1, replica_groups=mesh['dp'=8,'chip_x'=4,'chip_y'=4,'core'=2] {'chip_x','chip_y','core'}, dimensions={0} | all-to-all | bytes 1048576 | tf_op jit(solution)/shard_map/all_to_all | solution.py:247
  22.4 1.8 %forward.1 = (bf16[1024,256]{1,0:T(8,128)(2,1)S(1)}, f32[2,1024,128]{2,1,0:T(8,128)S(1)}, f32[2,1024,128]{2,1,0:T(8,128)S(1)}) custom-call(bf16[1024,256]{1,0:T(8,128)(2,1)S(1)} %bitcast.18, bf16[2,256,256]{2,1,0:T(8,128)(2,1)S(1)} %get-tuple-element.19.left_ref, bf16[4,128,128]{2,1,0:T(8,128)(2,1)S(1)} %get-tuple-element.20.right_ref, ...), custom_call_target="tpu_custom_call" | custom-call | flops 360972288 | bytes 2654208 | tf_op jit(solution)/shard_map/forward/pallas_call | solution.py:291
  24.2 13.2 %all_to_all.41.clip_ref = bf16[16,64,256]{2,1,0:T(8,128)(2,1)S(1)} all-to-all(bf16[16,64,256]{2,1,0:T(8,128)(2,1)S(1)} %bitcast.22), channel_id=1, replica_groups=mesh['dp'=8,'chip_x'=4,'chip_y'=4,'core'=2] {'chip_x','chip_y'}, dimensions={0} | all-to-all | bytes 1048576 | tf_op jit(solution)/shard_map/all_to_all | solution.py:247
  37.4 0.0 collective-permute-done.other_ref
  37.4 0.0 slice-start
  37.4 0.0 slice-start.1
  37.4 10.2 %project.1 = bf16[128,5120]{1,0:T(8,128)(2,1)S(1)} custom-call(s32[3]{0:T(128)S(1)} %pad_add_fusion.place_ref, bf16[16,64,256]{2,1,0:T(8,128)(2,1)S(1)} %all_to_all.41.clip_ref, bf16[864,5120]{1,0:T(8,128)(2,1)} %own_ref.3, bf16[864,5120]{1,0:T(8,128)(2,1)} %collective-permute-done.other_ref), custom_call_target="tpu_custom_call" | custom-call | flops 2264924160 | bytes 17694720 | tf_op jit(solution)/shard_map/project/pallas_call | solution.py:303
  47.6 0.0 slice-start.2
  47.6 21.1 %all_to_all.42.parts_ref = bf16[16,8,5120]{2,1,0:T(8,128)(2,1)S(1)} all-to-all(bf16[16,8,5120]{2,1,0:T(8,128)(2,1)S(1)} %bitcast.16), channel_id=1, replica_groups=mesh['dp'=8,'chip_x'=4,'chip_y'=4,'core'=2] {'chip_x','chip_y'}, dimensions={0} | all-to-all | bytes 2621440 | tf_op jit(solution)/shard_map/all_to_all | solution.py:247
  68.7 1.6 residual.1
  70.3 20.2 %all_to_all.43 = bf16[16,8,5120]{2,1,0:T(8,128)(2,1)S(1)} all-to-all(bf16[16,8,5120]{2,1,0:T(8,128)(2,1)S(1)} %residual.1), channel_id=1, replica_groups=mesh['dp'=8,'chip_x'=4,'chip_y'=4,'core'=2] {'chip_x','chip_y'}, dimensions={0} | all-to-all | bytes 2621440 | tf_op jit(solution)/shard_map/all_to_all | solution.py:247
  90.6 0.0 slice-done
  90.6 0.0 slice-done.1
  90.6 0.0 slice-done.2
  90.6 10.4 %back_project.1 = bf16[16,64,256]{2,1,0:T(8,128)(2,1)S(1)} custom-call(s32[3]{0:T(128)S(1)} %pad_add_fusion.place_ref, bf16[128,5120]{1,0:T(8,128)(2,1)S(1)} %bitcast.15, bf16[864,5120]{1,0:T(8,128)(2,1)S(1)} %bitcast.14, bf16[864,5120]{1,0:T(8,128)(2,1)} %collective-permute-done.other_ref), custom_call_target="tpu_custom_call" | custom-call | flops 2264924160 | bytes 17694720 | tf_op jit(solution)/shard_map/back_project/pallas_call | solution.py:331
  101.0 12.6 %all_to_all.44 = bf16[16,64,256]{2,1,0:T(8,128)(2,1)S(1)} all-to-all(bf16[16,64,256]{2,1,0:T(8,128)(2,1)S(1)} %back_project.1), channel_id=1, replica_groups=mesh['dp'=8,'chip_x'=4,'chip_y'=4,'core'=2] {'chip_x','chip_y'}, dimensions={0} | all-to-all | bytes 1048576 | tf_op jit(solution)/shard_map/all_to_all | solution.py:247
  113.6 1.6 backward.1
  115.2 21.5 %all_to_all.45 = bf16[32,40,256]{2,1,0:T(8,128)(2,1)S(1)} all-to-all(bf16[32,40,256]{2,1,0:T(8,128)(2,1)S(1)} %backward.1), channel_id=1, replica_groups=mesh['dp'=8,'chip_x'=4,'chip_y'=4,'core'=2] {'chip_x','chip_y','core'}, dimensions={0} | all-to-all | bytes 1310720 | tf_op jit(solution)/shard_map/all_to_all | solution.py:247
  136.7 1.5 input_grad.1
  138.2 15.3 %all_to_all.46.parts_ref = f32[8,8,256]{2,1,0:T(8,128)S(1)} all-to-all(f32[8,8,256]{2,1,0:T(8,128)S(1)} %get-tuple-element.25), channel_id=1, replica_groups=mesh['dp'=8,'chip_x'=4,'chip_y'=4,'core'=2] {'dp'}, dimensions={0} | all-to-all | bytes 131072 | tf_op jit(solution)/shard_map/all_to_all | solution.py:247
  153.6 13.9 %all_to_all.47.parts_ref = f32[32,8,256]{2,1,0:T(8,128)S(1)} all-to-all(f32[32,8,256]{2,1,0:T(8,128)S(1)} %sum_and_copy.1), channel_id=1, replica_groups=mesh['dp'=8,'chip_x'=4,'chip_y'=4,'core'=2] {'chip_x','chip_y','core'}, dimensions={0} | all-to-all | bytes 524288 | tf_op jit(solution)/shard_map/all_to_all | solution.py:247
  167.5 0.8 unpack.1
  (2 shorter events, 0.0 us)
Async XLA Ops:
  0.6 36.8 %collective-permute-start = (bf16[864,5120]{1,0:T(8,128)(2,1)}, bf16[864,5120]{1,0:T(8,128)(2,1)}, u32[]{:S(2)}, u32[]{:S(2)}) collective-permute-start(bf16[864,5120]{1,0:T(8,128)(2,1)} %own_ref.3), channel_id=1, source_target_pairs={{0,1},{1,0},{2,3},{3,2},{4,5},{5,4},{6,7},{7,6},{8,9},{9,8},{10,11... | collective-permute-start | bytes 26542088 | tf_op jit(solution)/shard_map/ppermute | solution.py:263
  37.4 53.2 %slice-start = ((s8[8847360]{0:T(1024)(128)(4,1)}), s8[4194304]{0:T(1024)(128)(4,1)S(1)}, s32[]{:S(2)}) async-start(s8[8847360]{0:T(1024)(128)(4,1)} %bitcast.13), calls=%async_computation.8 | async-start | bytes 8388608
  37.4 53.2 %slice-start.1 = ((s8[8847360]{0:T(1024)(128)(4,1)}), s8[4194304]{0:T(1024)(128)(4,1)S(1)}, s32[]{:S(2)}) async-start(s8[8847360]{0:T(1024)(128)(4,1)} %bitcast.13), calls=%async_computation.9 | async-start | bytes 8388608
  47.6 43.0 %slice-start.2 = ((s8[8847360]{0:T(1024)(128)(4,1)}), s8[458752]{0:T(1024)(128)(4,1)S(1)}, s32[]{:S(2)}) async-start(s8[8847360]{0:T(1024)(128)(4,1)} %bitcast.13), calls=%async_computation.10 | async-start | bytes 917504

commit v3 on v2

--- a/solution.py
+++ b/solution.py
@@ -101,7 +101,7 @@
     scale_ref[1] = 1.0 / scale
 
 
-def forward_kernel(x_ref, left_ref, right_ref, scale_ref, clip_ref, slope_ref, mixed_ref, hold_ref):
+def forward_kernel(place_ref, x_ref, left_ref, right_ref, scale_ref, clip_ref, slope_ref, mixed_ref, hold_ref):
     right_count = right_ref.shape[1]
     x = x_ref[...]
     mixed = dot(x, left_ref[0], NN) + dot(x, left_ref[1], NN)
@@ -114,21 +114,41 @@
         bounded = jnp.tanh(rotated * inverse)
         put_token(hold_ref, t, scale * bounded)
         put_token(slope_ref, t, 1.0 - bounded * bounded)
-    clip_ref[...] = joined(hold_ref).astype(BF16)
-
-
-def project_kernel(width, place_ref, clip_ref, own_ref, other_ref, o_ref):
-    core = place_ref[0]
-    chips = clip_ref.shape[0]
-    each = own_ref.shape[0] // width
-    total = None
-    for ref, base in ((own_ref, core * each), (other_ref, (1 - core) * each)):
-        for j in range(each):
-            start = pl.multiple_of((base + j) * TOK, TOK)
-            part = clip_ref[:, pl.ds(start, TOK), :].reshape(chips * TOK, WIDE)
-            term = dot(part[:, :width], ref[j * width : (j + 1) * width, :], NN)
-            total = term if total is None else total + term
-    o_ref[...] = total.astype(BF16)
+    chips, _, joint = clip_ref.shape
+    each = right_count // chips // 2
+    width = joint // each // 2
+    for chip in range(chips):
+        parts = []
+        for side in range(2):
+            base = chip * 2 * each + lax.rem(place_ref[0] + side, 2) * each
+            for j in range(each):
+                rows = pl.ds(pl.multiple_of((base + j) * TOK, TOK), TOK)
+                parts += [hold_ref[0, rows, :], hold_ref[1, rows, :][:, : width - LANES]]
+        clip_ref[chip] = jnp.concatenate(parts, axis=1).astype(BF16)
+
+
+def project_kernel(clip_ref, own_hbm, other_hbm, o_ref, near_ref, sems):
+    chips, _, depth = clip_ref.shape
+    hidden, columns = own_hbm.shape
+    block = columns // sems.shape[0]
+    cuts = [pl.ds(i * block, block) for i in range(sems.shape[0])]
+    copies = [
+        [
+            pltpu.make_async_copy(
+                ref.at[:, cut], near_ref.at[pl.ds(side * hidden, hidden), cut], sems.at[i, side]
+            )
+            for side, ref in enumerate((own_hbm, other_hbm))
+        ]
+        for i, cut in enumerate(cuts)
+    ]
+    for pair in copies:
+        for copy in pair:
+            copy.start()
+    part = clip_ref[...].reshape(chips * TOK, depth)
+    for cut, pair in zip(cuts, copies):
+        for copy in pair:
+            copy.wait()
+        o_ref[:, cut] = dot(part, near_ref[:, cut], NN).astype(BF16)
 
 
 def residual_kernel(place_ref, parts_ref, target_hbm, o_ref, rows_ref, sem):
@@ -142,27 +162,6 @@
     own = jnp.where(place_ref[2] == 1, rows[TOK:], rows[:TOK])
     grad = (total - own).astype(BF16)
     o_ref[...] = jnp.broadcast_to(grad[None], o_ref.shape)
-
-
-def back_project_kernel(place_ref, grad_ref, own_ref, other_ref, o_ref):
-    step = pl.program_id(0)
-    each = pl.num_programs(0) // 2
-    core = place_ref[0]
-    chips = o_ref.shape[0]
-
-    def put(ref, index):
-        part = dot(grad_ref[...], ref[...], NT)
-        part = widened(part, part.shape[0]).astype(BF16)
-        start = pl.multiple_of(index * TOK, TOK)
-        o_ref[:, pl.ds(start, TOK), :] = part.reshape(chips, TOK, WIDE)
-
-    @pl.when(step < each)
-    def _():
-        put(own_ref, core * each + step)
-
-    @pl.when(step >= each)
-    def _():
-        put(other_ref, (1 - core) * each + step - each)
 
 
 def packed_factors(width, grad_left, grad_right):
@@ -182,13 +181,22 @@
     return jnp.concatenate([*pieces, bottom], axis=0)
 
 
-def backward_kernel(width, grad_ref, slope_ref, mixed_ref, x_ref, right_ref, o_ref, hold_ref, back_ref):
+def backward_kernel(width, place_ref, grad_ref, slope_ref, mixed_ref, x_ref, right_ref, o_ref, hold_ref, back_ref):
     right_count = right_ref.shape[1]
     owners = o_ref.shape[0]
     own_rows = x_ref.shape[0] // owners
-    for side in range(2):
-        lanes = slice(side * LANES, (side + 1) * LANES)
-        hold_ref[side] = grad_ref[:, lanes].astype(F32) * slope_ref[side]
+    chips, _, joint = grad_ref.shape
+    each = joint // width // 2
+    for chip in range(chips):
+        rows_of_chip = grad_ref[chip].astype(F32)
+        for side in range(2):
+            base = chip * 2 * each + lax.rem(place_ref[0] + side, 2) * each
+            for j in range(each):
+                rows = pl.ds(pl.multiple_of((base + j) * TOK, TOK), TOK)
+                start = (side * each + j) * width
+                part = widened(rows_of_chip[:, start : start + width], TOK)
+                hold_ref[0, rows, :] = part[:, :LANES] * slope_ref[0, rows, :]
+                hold_ref[1, rows, :] = part[:, LANES:] * slope_ref[1, rows, :]
     right = right_ref[0], right_ref[1]
     grad_right = None
     for t in range(TOK):
@@ -257,6 +265,7 @@
     half = tokens // 2
     rows = right_count * TOK
     core = lax.axis_index("core")
+    smem = pl.BlockSpec(memory_space=pltpu.SMEM)
     slot = core * chips + lax.axis_index(CHIPS)
     place = jnp.stack([core, slot // 2, slot % 2])
 
@@ -290,31 +299,24 @@
     hold = pltpu.VMEM((2, rows, LANES), F32)
     clipped, slope, mixed = call(
         forward_kernel,
-        (shape(rows, WIDE), lanes_apart, lanes_apart),
+        (shape(chips, TOK, 2 * hidden), lanes_apart, lanes_apart),
         "forward",
         4 * rows * width * width + 6 * rows * width * right_count,
         12 * rows * width,
+        in_specs=[smem, *[pl.BlockSpec()] * 4],
         scratch_shapes=[hold],
-    )(moved, left_parts, right_parts, scales)
-    clipped_back = exchange(clipped.reshape(chips, 2 * each * TOK, WIDE), CHIPS)
-
-    block = 1024
-    smem = pl.BlockSpec(memory_space=pltpu.SMEM)
-    partial_out = call(
-        functools.partial(project_kernel, width),
-        shape(half, columns),
+    )(place, moved, left_parts, right_parts, scales)
+    clipped_back = exchange(clipped, CHIPS)
+    partial_out, near_rows = call(
+        project_kernel,
+        (shape(half, columns), shape(2 * hidden, columns)),
         "project",
         4 * half * hidden * columns,
         4 * hidden * columns,
-        grid=(columns // block,),
-        in_specs=[
-            smem,
-            pl.BlockSpec((chips, 2 * each * TOK, WIDE), lambda i: (0, 0, 0)),
-            pl.BlockSpec((hidden, block), lambda i: (0, i)),
-            pl.BlockSpec((hidden, block), lambda i: (0, i)),
-        ],
-        out_specs=pl.BlockSpec((half, block), lambda i: (0, i)),
-    )(place, clipped_back, in_hbm(weight_rows), in_hbm(other_rows))
+        vmem=24,
+        in_specs=[pl.BlockSpec(), *[pl.BlockSpec(memory_space=HBM)] * 2],
+        scratch_shapes=[pltpu.SemaphoreType.DMA((5, 2))],
+    )(clipped_back, in_hbm(weight_rows), in_hbm(other_rows))
     arrived = exchange(partial_out.reshape(chips, TOK, columns), CHIPS)
 
     grad_copies = call(
@@ -328,22 +330,8 @@
     )(place, arrived, in_hbm(target))
     out_grad = exchange(grad_copies, CHIPS).reshape(half, columns)
 
-    clipped_grad = call(
-        back_project_kernel,
-        shape(chips, 2 * each * TOK, WIDE),
-        "back_project",
-        4 * half * hidden * columns,
-        4 * hidden * columns,
-        grid=(2 * each,),
-        in_specs=[
-            smem,
-            pl.BlockSpec((half, columns), lambda i: (0, 0)),
-            pl.BlockSpec((width, columns), lambda i: (jnp.minimum(i, each - 1), 0)),
-            pl.BlockSpec((width, columns), lambda i: (jnp.maximum(i - each, 0), 0)),
-        ],
-        out_specs=pl.BlockSpec((chips, 2 * each * TOK, WIDE), lambda i: (0, 0, 0)),
-    )(place, out_grad, weight_rows, other_rows)
-    grad_owned = exchange(clipped_grad, CHIPS).reshape(rows, WIDE)
+    clipped_grad = dot(out_grad, near_rows, NT).astype(BF16)
+    grad_owned = exchange(clipped_grad.reshape(chips, TOK, 2 * hidden), CHIPS)
 
     per_owner = (each + 1) * TOK
     packed = call(
@@ -352,8 +340,9 @@
         "backward",
         4 * rows * width * width + 12 * rows * width * right_count,
         14 * rows * width,
+        in_specs=[smem, *[pl.BlockSpec()] * 5],
         scratch_shapes=[hold, hold],
-    )(grad_owned, slope, mixed, moved, right_parts)
+    )(place, grad_owned, slope, mixed, moved, right_parts)
     back = exchange(packed, TENSOR).reshape(chips, 2, per_owner, WIDE)
 
     groups = lax.axis_size("dp")

time: 169 us -> 162 us (0.959)
  Pallas kernels: 29.4 us -> 17.2 us
  matrix products: 0 us -> 5.53 us
    pallas_call x3 -> x2, Pallas kernels: 22.4 us -> 9.45 us  [the longest x1 6.91 us: local(): call(project_kernel, (shape(half, columns), shape(2 * hidden, columns)),...]
    dot_general x0 -> x1, matrix products: none -> 5.53 us  [dot(): return lax.dot_general(a, b, dims, preferred_element_type=F32)]
where the time goes in v3:
time: 162 us
  blocking collectives  134 us (83%)
  Pallas kernels  17.2 us (11%)
  matrix products  5.53 us (3%)
  starting transfers between devices  3.33 us (2%)
    all_to_all x8, blocking collectives, exchange(): return lax.all_to_all(array, axes, split_axis=0, concat_axis=0, tiled=True)  134 us
    pallas_call x1, Pallas kernels, local(): call(project_kernel, (shape(half, columns), shape(2 * hidden, columns)),...  6.91 us
    dot_general x1, matrix products, dot(): return lax.dot_general(a, b, dims, preferred_element_type=F32)  5.53 us
    ppermute x1, starting transfers between devices, local(): other_rows = lax.ppermute(weight_rows, 'core', [(0, 1), (1, 0)])  3.33 us
  transfers between devices with their start and end apart: 1, of which 0 were waited for; matrix products, arithmetic and copies ran while one was open for 0% of the time, Pallas kernels for 2%

profile of v3, /device:TPU:1, one launch (start us, length us, event | category | flops | bytes accessed | tf_op | source)
XLA Modules:
  0.0 161.5 jit_solution(17166535830494507195)
XLA Ops:
  0.6 3.3 %collective-permute-start = (bf16[864,5120]{1,0:T(8,128)(2,1)}, bf16[864,5120]{1,0:T(8,128)(2,1)}, u32[]{:S(2)}, u32[]{:S(2)}) collective-permute-start(bf16[864,5120]{1,0:T(8,128)(2,1)} %own_hbm.1), channel_id=1, source_target_pairs={{0,1},{1,0},{2,3},{3,2},{4,5},{5,4},{6,7},{7,6},{8,9},{9,8},{10,11... | collective-permute-start | bytes 26542088 | tf_op jit(solution)/shard_map/ppermute | solution.py:272
  4.0 1.4 first.1
  5.4 0.1 pad_add_fusion.place_ref
  5.5 16.9 %all_to_all.40 = bf16[32,32,256]{2,1,0:T(8,128)(2,1)S(1)} all-to-all(bf16[32,32,256]{2,1,0:T(8,128)(2,1)S(1)} %bitcast.19), channel_id=1, replica_groups=mesh['dp'=8,'chip_x'=4,'chip_y'=4,'core'=2] {'chip_x','chip_y','core'}, dimensions={0} | all-to-all | bytes 1048576 | tf_op jit(solution)/shard_map/all_to_all | solution.py:255
  22.4 2.5 %forward.1 = (bf16[16,8,1728]{2,1,0:T(8,128)(2,1)S(1)}, f32[2,1024,128]{2,1,0:T(8,128)S(1)}, f32[2,1024,128]{2,1,0:T(8,128)S(1)}) custom-call(s32[3]{0:T(128)S(1)} %pad_add_fusion.place_ref, bf16[1024,256]{1,0:T(8,128)(2,1)S(1)} %bitcast.16, bf16[2,256,256]{2,1,0:T(8,128)(2,1)S(1)} %get-tuple-element.21.left_ref, ...), custom_call_target="tpu_custom_call" | custom-call | flops 360972288 | bytes 2654208 | tf_op jit(solution)/shard_map/forward/pallas_call | solution.py:300
  24.9 12.7 %all_to_all.41.clip_ref = bf16[16,8,1728]{2,1,0:T(8,128)(2,1)S(1)} all-to-all(bf16[16,8,1728]{2,1,0:T(8,128)(2,1)S(1)} %get-tuple-element.24), channel_id=1, replica_groups=mesh['dp'=8,'chip_x'=4,'chip_y'=4,'core'=2] {'chip_x','chip_y'}, dimensions={0} | all-to-all | bytes 884736 | tf_op jit(solution)/shard_map/all_to_all | solution.py:255
  37.6 0.0 collective-permute-done.other_hbm
  37.6 6.9 %project.1 = (bf16[128,5120]{1,0:T(8,128)(2,1)S(1)}, bf16[1728,5120]{1,0:T(8,128)(2,1)S(1)}) custom-call(bf16[16,8,1728]{2,1,0:T(8,128)(2,1)S(1)} %all_to_all.41.clip_ref, bf16[864,5120]{1,0:T(8,128)(2,1)} %own_hbm.1, bf16[864,5120]{1,0:T(8,128)(2,1)} %collective-permute-done.other_hbm), custom_call_target="tpu_custom_call" | custom-call | flops 2264924160 | bytes 17694720 | tf_op jit(solution)/shard_map/project/pallas_call | solution.py:310
  44.5 20.8 %all_to_all.42.parts_ref = bf16[16,8,5120]{2,1,0:T(8,128)(2,1)S(1)} all-to-all(bf16[16,8,5120]{2,1,0:T(8,128)(2,1)S(1)} %bitcast.18), channel_id=1, replica_groups=mesh['dp'=8,'chip_x'=4,'chip_y'=4,'core'=2] {'chip_x','chip_y'}, dimensions={0} | all-to-all | bytes 2621440 | tf_op jit(solution)/shard_map/all_to_all | solution.py:255
  65.3 1.6 residual.1
  66.9 20.2 %all_to_all.43 = bf16[16,8,5120]{2,1,0:T(8,128)(2,1)S(1)} all-to-all(bf16[16,8,5120]{2,1,0:T(8,128)(2,1)S(1)} %residual.1), channel_id=1, replica_groups=mesh['dp'=8,'chip_x'=4,'chip_y'=4,'core'=2] {'chip_x','chip_y'}, dimensions={0} | all-to-all | bytes 2621440 | tf_op jit(solution)/shard_map/all_to_all | solution.py:255
  87.2 5.5 %convolution_convert_fusion = bf16[128,1728]{0,1:T(8,128)(2,1)} fusion(bf16[1728,5120]{1,0:T(8,128)(2,1)S(1)} %get-tuple-element.26, bf16[16,8,5120]{2,1,0:T(8,128)(2,1)S(1)} %all_to_all.43), kind=kOutput, calls=%fused_computation | convolution fusion | flops 2265145344 | bytes 19447808 | tf_op jit(solution)/shard_map/dot_general | solution.py:44
  92.7 1.2 copy.9
  93.9 12.3 %all_to_all.44.grad_ref = bf16[16,8,1728]{2,1,0:T(8,128)(2,1)S(1)} all-to-all(bf16[16,8,1728]{2,1,0:T(8,128)(2,1)S(1)} %bitcast.20), channel_id=1, replica_groups=mesh['dp'=8,'chip_x'=4,'chip_y'=4,'core'=2] {'chip_x','chip_y'}, dimensions={0} | all-to-all | bytes 884736 | tf_op jit(solution)/shard_map/all_to_all | solution.py:255
  106.2 2.4 %backward.1 = bf16[32,40,256]{2,1,0:T(8,128)(2,1)S(1)} custom-call(s32[3]{0:T(128)S(1)} %pad_add_fusion.place_ref, bf16[16,8,1728]{2,1,0:T(8,128)(2,1)S(1)} %all_to_all.44.grad_ref, f32[2,1024,128]{2,1,0:T(8,128)S(1)} %get-tuple-element.27.slope_ref, f32[2,1024,128]{2,1,0:T(8,128)S(1)} %get-tuple-element.28.mixed_ref, bf16[1024,256]{1,0:T(8,128)(2,1)S(1)} %bitcast.17, ...), custom_call_target="tpu_custom_call" | custom-call | flops 530841600 | bytes 3096576 | tf_op jit(solution)/shard_map/backward/pallas_call | solution.py:337
  108.6 21.5 %all_to_all.45 = bf16[32,40,256]{2,1,0:T(8,128)(2,1)S(1)} all-to-all(bf16[32,40,256]{2,1,0:T(8,128)(2,1)S(1)} %backward.1), channel_id=1, replica_groups=mesh['dp'=8,'chip_x'=4,'chip_y'=4,'core'=2] {'chip_x','chip_y','core'}, dimensions={0} | all-to-all | bytes 1310720 | tf_op jit(solution)/shard_map/all_to_all | solution.py:255
  130.0 1.5 input_grad.1
  131.6 15.3 %all_to_all.46.parts_ref = f32[8,8,256]{2,1,0:T(8,128)S(1)} all-to-all(f32[8,8,256]{2,1,0:T(8,128)S(1)} %get-tuple-element.29), channel_id=1, replica_groups=mesh['dp'=8,'chip_x'=4,'chip_y'=4,'core'=2] {'dp'}, dimensions={0} | all-to-all | bytes 131072 | tf_op jit(solution)/shard_map/all_to_all | solution.py:255
  146.9 13.9 %all_to_all.47.parts_ref = f32[32,8,256]{2,1,0:T(8,128)S(1)} all-to-all(f32[32,8,256]{2,1,0:T(8,128)S(1)} %sum_and_copy.1), channel_id=1, replica_groups=mesh['dp'=8,'chip_x'=4,'chip_y'=4,'core'=2] {'chip_x','chip_y','core'}, dimensions={0} | all-to-all | bytes 524288 | tf_op jit(solution)/shard_map/all_to_all | solution.py:255
  160.8 0.8 unpack.1
  (1 shorter events, 0.0 us)
Async XLA Ops:
  0.6 37.0 %collective-permute-start = (bf16[864,5120]{1,0:T(8,128)(2,1)}, bf16[864,5120]{1,0:T(8,128)(2,1)}, u32[]{:S(2)}, u32[]{:S(2)}) collective-permute-start(bf16[864,5120]{1,0:T(8,128)(2,1)} %own_hbm.1), channel_id=1, source_target_pairs={{0,1},{1,0},{2,3},{3,2},{4,5},{5,4},{6,7},{7,6},{8,9},{9,8},{10,11... | collective-permute-start | bytes 26542088 | tf_op jit(solution)/shard_map/ppermute | solution.py:272

commit v4 on v3

--- a/solution.py
+++ b/solution.py
@@ -164,6 +164,10 @@
     o_ref[...] = jnp.broadcast_to(grad[None], o_ref.shape)
 
 
+def turn_kernel(x_ref, o_ref):
+    o_ref[...] = x_ref[...].T
+
+
 def packed_factors(width, grad_left, grad_right):
     low = WIDE - width
     rest = widened(grad_right[2 * low :], grad_right.shape[0] - 2 * low)
@@ -295,13 +299,14 @@
     by_token, place = lax.optimization_barrier((by_token, place))
     moved = exchange(by_token.reshape(owners, each * TOK, WIDE), TENSOR).reshape(rows, WIDE)
 
+    moved, other_rows = lax.optimization_barrier((moved, other_rows))
     lanes_apart = shape(2, rows, LANES, dtype=F32)
     hold = pltpu.VMEM((2, rows, LANES), F32)
     clipped, slope, mixed = call(
         forward_kernel,
         (shape(chips, TOK, 2 * hidden), lanes_apart, lanes_apart),
         "forward",
-        4 * rows * width * width + 6 * rows * width * right_count,
+        10**10,
         12 * rows * width,
         in_specs=[smem, *[pl.BlockSpec()] * 4],
         scratch_shapes=[hold],
@@ -314,9 +319,9 @@
         4 * half * hidden * columns,
         4 * hidden * columns,
         vmem=24,
-        in_specs=[pl.BlockSpec(), *[pl.BlockSpec(memory_space=HBM)] * 2],
+        in_specs=[pl.BlockSpec(), *[pl.BlockSpec(memory_space=pl.ANY)] * 2],
         scratch_shapes=[pltpu.SemaphoreType.DMA((5, 2))],
-    )(clipped_back, in_hbm(weight_rows), in_hbm(other_rows))
+    )(clipped_back, weight_rows, in_hbm(other_rows))
     arrived = exchange(partial_out.reshape(chips, TOK, columns), CHIPS)
 
     grad_copies = call(
@@ -330,7 +335,10 @@
     )(place, arrived, in_hbm(target))
     out_grad = exchange(grad_copies, CHIPS).reshape(half, columns)
 
-    clipped_grad = dot(out_grad, near_rows, NT).astype(BF16)
+    turned_grad = dot(near_rows, out_grad, NT).astype(BF16)
+    clipped_grad = call(
+        turn_kernel, shape(half, 2 * hidden), "turn", 0, 8 * half * hidden
+    )(turned_grad)
     grad_owned = exchange(clipped_grad.reshape(chips, TOK, 2 * hidden), CHIPS)
 
     per_owner = (each + 1) * TOK

time: 162 us -> 159 us (0.981)
    pallas_call x1, Pallas kernels: 6.91 us -> 5.14 us  [local(): call(project_kernel, (shape(half, columns), shape(2 * hidden, columns)),...]
  transfers between devices with their start and end apart: 1 -> 1, of which waited for: 0 -> 0; matrix products, arithmetic and copies ran while one was open for 0% -> 0% of each run, Pallas kernels for 2% -> 1%
where the time goes in v4:
time: 159 us; the launch traced here: 158 us
  blocking collectives  134 us (84%)
  Pallas kernels  15.6 us (10%)
  matrix products  4.93 us (3%)
  starting transfers between devices  3.33 us (2%)
    all_to_all x8, blocking collectives, exchange(): return lax.all_to_all(array, axes, split_axis=0, concat_axis=0, tiled=True)  134 us
    pallas_call x1, Pallas kernels, local(): call(project_kernel, (shape(half, columns), shape(2 * hidden, columns)),...  5.14 us
    dot_general x1, matrix products, dot(): return lax.dot_general(a, b, dims, preferred_element_type=F32)  4.93 us
    ppermute x1, starting transfers between devices, local(): other_rows = lax.ppermute(weight_rows, 'core', [(0, 1), (1, 0)])  3.33 us
  transfers between devices with their start and end apart: 1, of which 0 were waited for; matrix products, arithmetic and copies ran while one was open for 0% of the time, Pallas kernels for 1%

profile of v4, /device:TPU:1, one launch (start us, length us, event | category | flops | bytes accessed | tf_op | source)
XLA Modules:
  0.0 158.2 jit_solution(10632754362719762517)
XLA Ops:
  0.6 3.3 %collective-permute-start = (bf16[864,5120]{1,0:T(8,128)(2,1)}, bf16[864,5120]{1,0:T(8,128)(2,1)}, u32[]{:S(2)}, u32[]{:S(2)}) collective-permute-start(bf16[864,5120]{1,0:T(8,128)(2,1)} %own_hbm.1), channel_id=1, source_target_pairs={{0,1},{1,0},{2,3},{3,2},{4,5},{5,4},{6,7},{7,6},{8,9},{9,8},{10,11... | collective-permute-start | bytes 26542088 | tf_op jit(solution)/shard_map/ppermute | solution.py:276
  4.0 1.4 first.1
  5.4 0.1 pad_add_fusion.place_ref
  5.5 16.9 %all_to_all.40 = bf16[32,32,256]{2,1,0:T(8,128)(2,1)S(1)} all-to-all(bf16[32,32,256]{2,1,0:T(8,128)(2,1)S(1)} %bitcast.22), channel_id=1, replica_groups=mesh['dp'=8,'chip_x'=4,'chip_y'=4,'core'=2] {'chip_x','chip_y','core'}, dimensions={0} | all-to-all | bytes 1048576 | tf_op jit(solution)/shard_map/all_to_all | solution.py:259
  22.4 0.0 collective-permute-done.other_hbm
  22.4 0.0 slice-start
  22.4 0.0 slice-start.1
  22.4 0.0 slice-start.2
  22.4 2.6 %forward.1 = (bf16[16,8,1728]{2,1,0:T(8,128)(2,1)S(1)}, f32[2,1024,128]{2,1,0:T(8,128)S(1)}, f32[2,1024,128]{2,1,0:T(8,128)S(1)}) custom-call(s32[3]{0:T(128)S(1)} %pad_add_fusion.place_ref, bf16[1024,256]{1,0:T(8,128)(2,1)S(1)} %bitcast.18, bf16[2,256,256]{2,1,0:T(8,128)(2,1)S(1)} %get-tuple-element.24.left_ref, ...), custom_call_target="tpu_custom_call" | custom-call | flops 10000000000 | bytes 2654208 | tf_op jit(solution)/shard_map/forward/pallas_call | solution.py:305
  24.9 12.7 %all_to_all.41.clip_ref = bf16[16,8,1728]{2,1,0:T(8,128)(2,1)S(1)} all-to-all(bf16[16,8,1728]{2,1,0:T(8,128)(2,1)S(1)} %get-tuple-element.27), channel_id=1, replica_groups=mesh['dp'=8,'chip_x'=4,'chip_y'=4,'core'=2] {'chip_x','chip_y'}, dimensions={0} | all-to-all | bytes 884736 | tf_op jit(solution)/shard_map/all_to_all | solution.py:259
  37.7 0.0 slice-done
  37.7 0.0 slice-done.1
  37.7 0.0 slice-done.2
  37.7 5.1 %project.1 = (bf16[128,5120]{1,0:T(8,128)(2,1)S(1)}, bf16[1728,5120]{1,0:T(8,128)(2,1)S(1)}) custom-call(bf16[16,8,1728]{2,1,0:T(8,128)(2,1)S(1)} %all_to_all.41.clip_ref, bf16[864,5120]{1,0:T(8,128)(2,1)S(1)} %bitcast.16, bf16[864,5120]{1,0:T(8,128)(2,1)} %collective-permute-done.other_hbm), custom_call_target="tpu_custom_call" | custom-call | flops 2264924160 | bytes 17694720 | tf_op jit(solution)/shard_map/project/pallas_call | solution.py:315
  42.8 20.8 %all_to_all.42.parts_ref = bf16[16,8,5120]{2,1,0:T(8,128)(2,1)S(1)} all-to-all(bf16[16,8,5120]{2,1,0:T(8,128)(2,1)S(1)} %bitcast.21), channel_id=1, replica_groups=mesh['dp'=8,'chip_x'=4,'chip_y'=4,'core'=2] {'chip_x','chip_y'}, dimensions={0} | all-to-all | bytes 2621440 | tf_op jit(solution)/shard_map/all_to_all | solution.py:259
  63.6 1.6 %residual.1 = bf16[16,8,5120]{2,1,0:T(8,128)(2,1)S(1)} custom-call(s32[3]{0:T(128)S(1)} %pad_add_fusion.place_ref, bf16[16,8,5120]{2,1,0:T(8,128)(2,1)S(1)} %all_to_all.42.parts_ref, bf16[256,5120]{1,0:T(8,128)(2,1)} %target_hbm.1), custom_call_target="tpu_custom_call" | custom-call | bytes 2621440 | tf_op jit(solution)/shard_map/residual/pallas_call | solution.py:327
  65.2 20.2 %all_to_all.43 = bf16[16,8,5120]{2,1,0:T(8,128)(2,1)S(1)} all-to-all(bf16[16,8,5120]{2,1,0:T(8,128)(2,1)S(1)} %residual.1), channel_id=1, replica_groups=mesh['dp'=8,'chip_x'=4,'chip_y'=4,'core'=2] {'chip_x','chip_y'}, dimensions={0} | all-to-all | bytes 2621440 | tf_op jit(solution)/shard_map/all_to_all | solution.py:259
  85.5 4.9 %convolution_convert_fusion.x_ref = bf16[1728,128]{1,0:T(8,128)(2,1)S(1)} fusion(bf16[1728,5120]{1,0:T(8,128)(2,1)S(1)} %get-tuple-element.29, bf16[16,8,5120]{2,1,0:T(8,128)(2,1)S(1)} %all_to_all.43), kind=kOutput, calls=%fused_computation | convolution fusion | flops 2265145344 | bytes 19447808 | tf_op jit(solution)/shard_map/dot_general | solution.py:44
  90.4 0.2 turn.1
  90.6 12.3 %all_to_all.44.grad_ref = bf16[16,8,1728]{2,1,0:T(8,128)(2,1)S(1)} all-to-all(bf16[16,8,1728]{2,1,0:T(8,128)(2,1)S(1)} %bitcast.20), channel_id=1, replica_groups=mesh['dp'=8,'chip_x'=4,'chip_y'=4,'core'=2] {'chip_x','chip_y'}, dimensions={0} | all-to-all | bytes 884736 | tf_op jit(solution)/shard_map/all_to_all | solution.py:259
  102.8 2.4 %backward.1 = bf16[32,40,256]{2,1,0:T(8,128)(2,1)S(1)} custom-call(s32[3]{0:T(128)S(1)} %pad_add_fusion.place_ref, bf16[16,8,1728]{2,1,0:T(8,128)(2,1)S(1)} %all_to_all.44.grad_ref, f32[2,1024,128]{2,1,0:T(8,128)S(1)} %get-tuple-element.31.slope_ref, f32[2,1024,128]{2,1,0:T(8,128)S(1)} %get-tuple-element.32.mixed_ref, bf16[1024,256]{1,0:T(8,128)(2,1)S(1)} %bitcast.19, ...), custom_call_target="tpu_custom_call" | custom-call | flops 530841600 | bytes 3096576 | tf_op jit(solution)/shard_map/backward/pallas_call | solution.py:345
  105.2 21.5 %all_to_all.45 = bf16[32,40,256]{2,1,0:T(8,128)(2,1)S(1)} all-to-all(bf16[32,40,256]{2,1,0:T(8,128)(2,1)S(1)} %backward.1), channel_id=1, replica_groups=mesh['dp'=8,'chip_x'=4,'chip_y'=4,'core'=2] {'chip_x','chip_y','core'}, dimensions={0} | all-to-all | bytes 1310720 | tf_op jit(solution)/shard_map/all_to_all | solution.py:259
  126.7 1.5 input_grad.1
  128.2 15.2 %all_to_all.46.parts_ref = f32[8,8,256]{2,1,0:T(8,128)S(1)} all-to-all(f32[8,8,256]{2,1,0:T(8,128)S(1)} %get-tuple-element.33), channel_id=1, replica_groups=mesh['dp'=8,'chip_x'=4,'chip_y'=4,'core'=2] {'dp'}, dimensions={0} | all-to-all | bytes 131072 | tf_op jit(solution)/shard_map/all_to_all | solution.py:259
  143.5 13.9 %all_to_all.47.parts_ref = f32[32,8,256]{2,1,0:T(8,128)S(1)} all-to-all(f32[32,8,256]{2,1,0:T(8,128)S(1)} %sum_and_copy.1), channel_id=1, replica_groups=mesh['dp'=8,'chip_x'=4,'chip_y'=4,'core'=2] {'chip_x','chip_y','core'}, dimensions={0} | all-to-all | bytes 524288 | tf_op jit(solution)/shard_map/all_to_all | solution.py:259
  157.4 0.8 unpack.1
  (2 shorter events, 0.0 us)
Async XLA Ops:
  0.6 21.7 %collective-permute-start = (bf16[864,5120]{1,0:T(8,128)(2,1)}, bf16[864,5120]{1,0:T(8,128)(2,1)}, u32[]{:S(2)}, u32[]{:S(2)}) collective-permute-start(bf16[864,5120]{1,0:T(8,128)(2,1)} %own_hbm.1), channel_id=1, source_target_pairs={{0,1},{1,0},{2,3},{3,2},{4,5},{5,4},{6,7},{7,6},{8,9},{9,8},{10,11... | collective-permute-start | bytes 26542088 | tf_op jit(solution)/shard_map/ppermute | solution.py:276
  22.4 15.3 %slice-start = ((s8[8847360]{0:T(1024)(128)(4,1)}), s8[4194304]{0:T(1024)(128)(4,1)S(1)}, s32[]{:S(2)}) async-start(s8[8847360]{0:T(1024)(128)(4,1)} %bitcast.15), calls=%async_computation.8 | async-start | bytes 8388608
  22.4 15.3 %slice-start.1 = ((s8[8847360]{0:T(1024)(128)(4,1)}), s8[4194304]{0:T(1024)(128)(4,1)S(1)}, s32[]{:S(2)}) async-start(s8[8847360]{0:T(1024)(128)(4,1)} %bitcast.15), calls=%async_computation.9 | async-start | bytes 8388608
  22.4 15.3 %slice-start.2 = ((s8[8847360]{0:T(1024)(128)(4,1)}), s8[458752]{0:T(1024)(128)(4,1)S(1)}, s32[]{:S(2)}) async-start(s8[8847360]{0:T(1024)(128)(4,1)} %bitcast.15), calls=%async_computation.10 | async-start | bytes 917504

commit v5 on v4

--- a/solution.py
+++ b/solution.py
@@ -44,9 +44,11 @@
     return lax.dot_general(a, b, dims, preferred_element_type=F32)
 
 
-def dot3(a, b, dims):
-    (a_high, a_low), (b_high, b_low) = a, b
-    return dot(a_high, b_high, dims) + (dot(a_high, b_low, dims) + dot(a_low, b_high, dims))
+def stacked_dot(a, b):
+    high, low = b
+    count = a.shape[0] // 2
+    both = dot(a, high, NN)
+    return both[:count] + (both[count:] + dot(a[:count], low, NN))
 
 
 def of_token(ref, token, count):
@@ -69,8 +71,8 @@
 
 
 def first_kernel(width, *refs):
-    *sources, o_ref, left_ref, right_ref, scale_ref = refs[:8]
-    *buffers, sems = refs[8:]
+    *sources, o_ref, left_ref, back_left_ref, right_ref, scale_ref = refs[:9]
+    *buffers, sems = refs[9:]
     x_hbm, x_buf = sources[0], buffers[0]
     count = x_hbm.shape[0] // width
     tall = 2 * width
@@ -93,79 +95,78 @@
     for copy in copies[count // 2 :]:
         copy.wait()
     _, left_buf, right_buf, scale_buf = buffers
-    left_ref[0], left_ref[1] = halves(widened(left_buf[...], WIDE))
-    right_ref[0], right_ref[1] = halves(right_buf[...])
-    right_ref[2], right_ref[3] = halves(right_buf[...].T)
+    high, low = halves(widened(left_buf[...], WIDE))
+    left_ref[:, :WIDE] = high
+    left_ref[:, WIDE:] = low
+    back_left_ref[...] = jnp.concatenate([high[:width], low[:width]], axis=0)
+    right_ref[0] = jnp.concatenate(halves(right_buf[...]), axis=0)
+    right_ref[1] = jnp.concatenate(halves(right_buf[...].T), axis=0)
     scale = widened(scale_buf[...].T, right_buf.shape[0], 1.0)
     scale_ref[0] = scale
     scale_ref[1] = 1.0 / scale
 
 
-def forward_kernel(place_ref, x_ref, left_ref, right_ref, scale_ref, clip_ref, slope_ref, mixed_ref, hold_ref):
-    right_count = right_ref.shape[1]
-    x = x_ref[...]
-    mixed = dot(x, left_ref[0], NN) + dot(x, left_ref[1], NN)
+def forward_kernel(x_ref, left_ref, right_ref, scale_ref, clip_ref, slope_ref, mixed_ref, hold_ref):
+    right_count = right_ref.shape[2]
+    both = dot(x_ref[...], left_ref[...], NN)
+    mixed = both[:, :WIDE] + both[:, WIDE:]
     mixed_ref[0] = mixed[:, :LANES]
     mixed_ref[1] = mixed[:, LANES:]
-    turned = right_ref[2], right_ref[3]
+    turned = right_ref[1]
     scale, inverse = scale_ref[0], scale_ref[1]
     for t in range(TOK):
-        rotated = dot3(turned, halves(of_token(mixed_ref, t, right_count)), NN)
+        rotated = stacked_dot(turned, halves(of_token(mixed_ref, t, right_count)))
         bounded = jnp.tanh(rotated * inverse)
         put_token(hold_ref, t, scale * bounded)
         put_token(slope_ref, t, 1.0 - bounded * bounded)
+    core = lax.axis_index("core")
     chips, _, joint = clip_ref.shape
     each = right_count // chips // 2
     width = joint // each // 2
     for chip in range(chips):
         parts = []
         for side in range(2):
-            base = chip * 2 * each + lax.rem(place_ref[0] + side, 2) * each
+            base = chip * 2 * each + lax.rem(core + side, 2) * each
             for j in range(each):
                 rows = pl.ds(pl.multiple_of((base + j) * TOK, TOK), TOK)
                 parts += [hold_ref[0, rows, :], hold_ref[1, rows, :][:, : width - LANES]]
         clip_ref[chip] = jnp.concatenate(parts, axis=1).astype(BF16)
 
 
-def project_kernel(clip_ref, own_hbm, other_hbm, o_ref, near_ref, sems):
+def own_slot(chips):
+    x, y = (lax.axis_index(axis) for axis in CHIPS)
+    return lax.axis_index("core") * chips + x * lax.axis_size(CHIPS[1]) + y
+
+
+def project_kernel(clip_ref, own_ref, other_ref, target_hbm, o_ref, rows_ref, sem):
     chips, _, depth = clip_ref.shape
-    hidden, columns = own_hbm.shape
-    block = columns // sems.shape[0]
-    cuts = [pl.ds(i * block, block) for i in range(sems.shape[0])]
-    copies = [
-        [
-            pltpu.make_async_copy(
-                ref.at[:, cut], near_ref.at[pl.ds(side * hidden, hidden), cut], sems.at[i, side]
-            )
-            for side, ref in enumerate((own_hbm, other_hbm))
-        ]
-        for i, cut in enumerate(cuts)
-    ]
-    for pair in copies:
-        for copy in pair:
-            copy.start()
-    part = clip_ref[...].reshape(chips * TOK, depth)
-    for cut, pair in zip(cuts, copies):
-        for copy in pair:
-            copy.wait()
-        o_ref[:, cut] = dot(part, near_ref[:, cut], NN).astype(BF16)
-
-
-def residual_kernel(place_ref, parts_ref, target_hbm, o_ref, rows_ref, sem):
+    hidden, columns = own_ref.shape
     pair = rows_ref.shape[0]
-    start = pl.multiple_of(place_ref[1] * pair, pair)
+    start = pl.multiple_of(own_slot(chips) // 2 * pair, pair)
     copy = pltpu.make_async_copy(target_hbm.at[pl.ds(start, pair)], rows_ref, sem)
     copy.start()
+    part = clip_ref[...].reshape(chips * TOK, depth)
+    own, other = part[:, :hidden], part[:, hidden:]
+    block = 1024
+    for i in range(columns // block):
+        cut = slice(i * block, (i + 1) * block)
+        total = dot(own, own_ref[:, cut], NN) + dot(other, other_ref[:, cut], NN)
+        o_ref[:, cut] = total.astype(BF16)
+    copy.wait()
+
+
+def residual_kernel(parts_ref, rows_ref, o_ref):
     total = jnp.sum(parts_ref[...].astype(F32), axis=0)
-    copy.wait()
     rows = rows_ref[...].astype(F32)
-    own = jnp.where(place_ref[2] == 1, rows[TOK:], rows[:TOK])
-    grad = (total - own).astype(BF16)
-    o_ref[...] = jnp.broadcast_to(grad[None], o_ref.shape)
-
-
-def turn_kernel(x_ref, o_ref):
-    o_ref[...] = x_ref[...].T
+    odd = lax.rem(own_slot(parts_ref.shape[0]), 2) == 1
+    own = jnp.where(odd, rows[TOK:], rows[:TOK])
+    o_ref[...] = jnp.broadcast_to((total - own).astype(BF16)[None], o_ref.shape)
+
+
+def turn_kernel(own_ref, other_ref, o_ref):
+    hidden = own_ref.shape[0]
+    o_ref[:, :hidden] = own_ref[...].T
+    o_ref[:, hidden:] = other_ref[...].T
 
 
 def packed_factors(width, grad_left, grad_right):
@@ -185,50 +186,55 @@
     return jnp.concatenate([*pieces, bottom], axis=0)
 
 
-def backward_kernel(width, place_ref, grad_ref, slope_ref, mixed_ref, x_ref, right_ref, o_ref, hold_ref, back_ref):
-    right_count = right_ref.shape[1]
+def backward_kernel(width, grad_ref, slope_ref, mixed_ref, x_ref, right_ref, o_ref, hold_ref, back_ref):
+    right_count = right_ref.shape[2]
     owners = o_ref.shape[0]
     own_rows = x_ref.shape[0] // owners
+    core = lax.axis_index("core")
     chips, _, joint = grad_ref.shape
     each = joint // width // 2
     for chip in range(chips):
         rows_of_chip = grad_ref[chip].astype(F32)
         for side in range(2):
-            base = chip * 2 * each + lax.rem(place_ref[0] + side, 2) * each
+            base = chip * 2 * each + lax.rem(core + side, 2) * each
             for j in range(each):
                 rows = pl.ds(pl.multiple_of((base + j) * TOK, TOK), TOK)
                 start = (side * each + j) * width
                 part = widened(rows_of_chip[:, start : start + width], TOK)
                 hold_ref[0, rows, :] = part[:, :LANES] * slope_ref[0, rows, :]
                 hold_ref[1, rows, :] = part[:, LANES:] * slope_ref[1, rows, :]
-    right = right_ref[0], right_ref[1]
+    right = right_ref[0]
     grad_right = None
     for t in range(TOK):
         rotated_grad = halves(of_token(hold_ref, t, right_count))
-        put_token(back_ref, t, dot3(right, rotated_grad, NN))
-        term = dot3(halves(of_token(mixed_ref, t, right_count)), rotated_grad, NT)
+        put_token(back_ref, t, stacked_dot(right, rotated_grad))
+        term = dot(of_token(mixed_ref, t, right_count).astype(BF16), rotated_grad[0], NT)
         grad_right = term if grad_right is None else grad_right + term
-    high, low = halves(joined(back_ref))
-    x = x_ref[...]
-    grad_left = dot(x, high, TN) + dot(x, low, TN)
-    o_ref[:, :own_rows, :] = high.reshape(owners, own_rows, WIDE)
+    mixed_grad = joined(back_ref).astype(BF16)
+    grad_left = dot(x_ref[...], mixed_grad, TN)
+    o_ref[:, :own_rows, :] = mixed_grad.reshape(owners, own_rows, WIDE)
     packed = packed_factors(width, grad_left, grad_right)
     o_ref[:, own_rows:, :] = packed.reshape(owners, TOK, WIDE).astype(BF16)
 
 
-def input_grad_kernel(width, back_ref, left_ref, o_ref, factor_ref):
+def input_grad_kernel(width, back_ref, left_ref, o_hbm, factor_ref, o_ref, sems):
     chips, _, total, _ = back_ref.shape
     count = total // TOK - 1
     half = chips * TOK
-    left_high, left_low = left_ref[0, :width], left_ref[1, :width]
+    copies = []
     for j in range(count):
-        for core in range(2):
-            part = back_ref[:, core, j * TOK : (j + 1) * TOK, :].reshape(half, WIDE)
-            o_ref[j * width : (j + 1) * width, core * half : (core + 1) * half] = dot(
-                left_high, part, NT
-            ) + dot(left_low, part, NT)
+        parts = [
+            back_ref[:, core, j * TOK : (j + 1) * TOK, :].reshape(half, WIDE) for core in range(2)
+        ]
+        both = dot(left_ref[...], jnp.concatenate(parts, axis=0), NT)
+        o_ref[j * width : (j + 1) * width, :] = both[:width] + both[width:]
+        cut = pl.ds(j * width, width)
+        copies.append(pltpu.make_async_copy(o_ref.at[cut], o_hbm.at[cut], sems.at[j]))
+        copies[j].start()
     factors = back_ref[:, :, count * TOK :, :].astype(F32)
     factor_ref[...] = jnp.broadcast_to(jnp.sum(factors, axis=(0, 1))[None], factor_ref.shape)
+    for copy in copies:
+        copy.wait()
 
 
 def sum_and_copy_kernel(parts_ref, o_ref):
@@ -268,20 +274,16 @@
     owners = 2 * chips
     half = tokens // 2
     rows = right_count * TOK
-    core = lax.axis_index("core")
-    smem = pl.BlockSpec(memory_space=pltpu.SMEM)
-    slot = core * chips + lax.axis_index(CHIPS)
-    place = jnp.stack([core, slot // 2, slot % 2])
-
     other_rows = lax.ppermute(weight_rows, "core", [(0, 1), (1, 0)])
 
     turned_x, turned_scale = activations.T, clip_scale.T
-    by_token, left_parts, right_parts, scales = call(
+    by_token, left_parts, back_left, right_parts, scales = call(
         functools.partial(first_kernel, width),
         (
             shape(chips, 2, each, TOK, WIDE),
-            shape(2, WIDE, WIDE),
-            shape(4, right_count, right_count),
+            shape(WIDE, 2 * WIDE),
+            shape(2 * width, WIDE),
+            shape(2, 2 * right_count, right_count),
             shape(2, right_count, WIDE, dtype=F32),
         ),
         "first",
@@ -296,7 +298,6 @@
             pltpu.SemaphoreType.DMA((each // 2 + 3,)),
         ],
     )(*map(in_hbm, (turned_x, left_factor, right_factor, turned_scale)))
-    by_token, place = lax.optimization_barrier((by_token, place))
     moved = exchange(by_token.reshape(owners, each * TOK, WIDE), TENSOR).reshape(rows, WIDE)
 
     moved, other_rows = lax.optimization_barrier((moved, other_rows))
@@ -308,20 +309,19 @@
         "forward",
         10**10,
         12 * rows * width,
-        in_specs=[smem, *[pl.BlockSpec()] * 4],
         scratch_shapes=[hold],
-    )(place, moved, left_parts, right_parts, scales)
+    )(moved, left_parts, right_parts, scales)
     clipped_back = exchange(clipped, CHIPS)
-    partial_out, near_rows = call(
+    partial_out, own_rows = call(
         project_kernel,
-        (shape(half, columns), shape(2 * hidden, columns)),
+        (shape(half, columns), shape(2 * TOK, columns)),
         "project",
         4 * half * hidden * columns,
         4 * hidden * columns,
         vmem=24,
-        in_specs=[pl.BlockSpec(), *[pl.BlockSpec(memory_space=pl.ANY)] * 2],
-        scratch_shapes=[pltpu.SemaphoreType.DMA((5, 2))],
-    )(clipped_back, weight_rows, in_hbm(other_rows))
+        in_specs=[*[pl.BlockSpec()] * 3, pl.BlockSpec(memory_space=HBM)],
+        scratch_shapes=[pltpu.SemaphoreType.DMA(())],
+    )(clipped_back, weight_rows, other_rows, in_hbm(target))
     arrived = exchange(partial_out.reshape(chips, TOK, columns), CHIPS)
 
     grad_copies = call(
@@ -330,15 +330,13 @@
         "residual",
         0,
         4 * half * columns,
-        in_specs=[smem, pl.BlockSpec(), pl.BlockSpec(memory_space=HBM)],
-        scratch_shapes=[pltpu.VMEM((2 * TOK, columns), BF16), pltpu.SemaphoreType.DMA(())],
-    )(place, arrived, in_hbm(target))
+    )(arrived, own_rows)
     out_grad = exchange(grad_copies, CHIPS).reshape(half, columns)
 
-    turned_grad = dot(near_rows, out_grad, NT).astype(BF16)
+    turned_grads = [dot(near, out_grad, NT).astype(BF16) for near in (weight_rows, other_rows)]
     clipped_grad = call(
         turn_kernel, shape(half, 2 * hidden), "turn", 0, 8 * half * hidden
-    )(turned_grad)
+    )(*turned_grads)
     grad_owned = exchange(clipped_grad.reshape(chips, TOK, 2 * hidden), CHIPS)
 
     per_owner = (each + 1) * TOK
@@ -348,9 +346,8 @@
         "backward",
         4 * rows * width * width + 12 * rows * width * right_count,
         14 * rows * width,
-        in_specs=[smem, *[pl.BlockSpec()] * 5],
         scratch_shapes=[hold, hold],
-    )(place, grad_owned, slope, mixed, moved, right_parts)
+    )(grad_owned, slope, mixed, moved, right_parts)
     back = exchange(packed, TENSOR).reshape(chips, 2, per_owner, WIDE)
 
     groups = lax.axis_size("dp")
@@ -360,7 +357,12 @@
         "input_grad",
         4 * tokens * hidden * width,
         6 * tokens * hidden,
-    )(back, left_parts)
+        out_specs=(pl.BlockSpec(memory_space=HBM), pl.BlockSpec()),
+        scratch_shapes=[
+            pltpu.VMEM((hidden, tokens), F32),
+            pltpu.SemaphoreType.DMA((each,)),
+        ],
+    )(back, back_left)
     factor_parts = exchange(factor_copies, "dp")
     factor_sums = call(
         sum_and_copy_kernel, shape(owners, TOK, WIDE, dtype=F32), "sum_and_copy", 0, 1 << 20

time: 159 us -> 154 us (0.969)
  Pallas kernels: 15.6 us -> 11.4 us
    dot_general x1 -> x2, matrix products: 4.93 us -> 4.9 us  [dot(): return lax.dot_general(a, b, dims, preferred_element_type=F32)]
where the time goes in v5:
time: 154 us
  blocking collectives  134 us (87%)
  Pallas kernels  11.4 us (7%)
  matrix products  4.9 us (3%)
  starting transfers between devices  3.33 us (2%)
    all_to_all x8, blocking collectives, exchange(): return lax.all_to_all(array, axes, split_axis=0, concat_axis=0, tiled=True)  134 us
    dot_general x2, matrix products, dot(): return lax.dot_general(a, b, dims, preferred_element_type=F32)  4.9 us
    pallas_call x1, Pallas kernels, local(): call(project_kernel, (shape(half, columns), shape(2 * TOK, columns)), 'pr...  3.71 us
    ppermute x1, starting transfers between devices, local(): other_rows = lax.ppermute(weight_rows, 'core', [(0, 1), (1, 0)])  3.33 us
  transfers between devices with their start and end apart: 1, of which 0 were waited for; matrix products, arithmetic and copies ran while one was open for 0% of the time, Pallas kernels for 1%

profile of v5, /device:TPU:1, one launch (start us, length us, event | category | flops | bytes accessed | tf_op | source)
XLA Modules:
  0.0 154.0 jit_solution(13921595204993508397)
XLA Ops:
  0.6 3.3 %collective-permute-start = (bf16[864,5120]{1,0:T(8,128)(2,1)}, bf16[864,5120]{1,0:T(8,128)(2,1)S(1)}, u32[]{:S(2)}, u32[]{:S(2)}) collective-permute-start(bf16[864,5120]{1,0:T(8,128)(2,1)} %own_ref.1), channel_id=1, source_target_pairs={{0,1},{1,0},{2,3},{3,2},{4,5},{5,4},{6,7},{7,6},{8,9},{9,8},{10,11... | collective-permute-start | bytes 26542088 | tf_op jit(solution)/shard_map/ppermute | solution.py:277
  4.0 1.4 first.1
  5.4 16.9 %all_to_all.40 = bf16[32,32,256]{2,1,0:T(8,128)(2,1)S(1)} all-to-all(bf16[32,32,256]{2,1,0:T(8,128)(2,1)S(1)} %bitcast.30), channel_id=1, replica_groups=mesh['dp'=8,'chip_x'=4,'chip_y'=4,'core'=2] {'chip_x','chip_y','core'}, dimensions={0} | all-to-all | bytes 1048576 | tf_op jit(solution)/shard_map/all_to_all | solution.py:265
  22.3 0.0 collective-permute-done.other_ref
  22.3 0.0 slice-start
  22.3 0.0 slice-start.1
  22.3 0.0 slice-start.2
  22.3 2.0 %forward.1 = (bf16[16,8,1728]{2,1,0:T(8,128)(2,1)S(1)}, f32[2,1024,128]{2,1,0:T(8,128)S(1)}, f32[2,1024,128]{2,1,0:T(8,128)S(1)}) custom-call(bf16[1024,256]{1,0:T(8,128)(2,1)S(1)} %bitcast.26, bf16[256,512]{1,0:T(8,128)(2,1)S(1)} %get-tuple-element.21.left_ref, bf16[2,256,128]{2,1,0:T(8,128)(2,1)S(1)} %get-tuple-element.22.right_ref, ...), custom_call_target="tpu_custom_call" | custom-call | flops 10000000000 | bytes 2654208 | tf_op jit(solution)/shard_map/forward/pallas_call | solution.py:306
  24.4 12.8 %all_to_all.41.clip_ref = bf16[16,8,1728]{2,1,0:T(8,128)(2,1)S(1)} all-to-all(bf16[16,8,1728]{2,1,0:T(8,128)(2,1)S(1)} %get-tuple-element.24), channel_id=1, replica_groups=mesh['dp'=8,'chip_x'=4,'chip_y'=4,'core'=2] {'chip_x','chip_y'}, dimensions={0} | all-to-all | bytes 884736 | tf_op jit(solution)/shard_map/all_to_all | solution.py:265
  37.2 0.0 slice-done
  37.2 0.0 slice-done.1
  37.2 0.0 slice-done.2
  37.2 3.7 %project.1 = (bf16[128,5120]{1,0:T(8,128)(2,1)S(1)}, bf16[16,5120]{1,0:T(8,128)(2,1)S(1)}) custom-call(bf16[16,8,1728]{2,1,0:T(8,128)(2,1)S(1)} %all_to_all.41.clip_ref, bf16[864,5120]{1,0:T(8,128)(2,1)S(1)} %bitcast.24, bf16[864,5120]{1,0:T(8,128)(2,1)S(1)} %collective-permute-done.other_ref, bf16[256,5120]{1,0:T(8,128)(2,1)} %target_hbm.1), custom_call_target="tpu_custom_call" | custom-call | flops 2264924160 | bytes 17694720 | tf_op jit(solution)/shard_map/project/pallas_call | solution.py:315
  40.9 20.8 %all_to_all.42.parts_ref = bf16[16,8,5120]{2,1,0:T(8,128)(2,1)S(1)} all-to-all(bf16[16,8,5120]{2,1,0:T(8,128)(2,1)S(1)} %bitcast.29), channel_id=1, replica_groups=mesh['dp'=8,'chip_x'=4,'chip_y'=4,'core'=2] {'chip_x','chip_y'}, dimensions={0} | all-to-all | bytes 2621440 | tf_op jit(solution)/shard_map/all_to_all | solution.py:265
  61.7 0.2 residual.1
  62.0 20.3 %all_to_all.43 = bf16[16,8,5120]{2,1,0:T(8,128)(2,1)S(1)} all-to-all(bf16[16,8,5120]{2,1,0:T(8,128)(2,1)S(1)} %residual.1), channel_id=1, replica_groups=mesh['dp'=8,'chip_x'=4,'chip_y'=4,'core'=2] {'chip_x','chip_y'}, dimensions={0} | all-to-all | bytes 2621440 | tf_op jit(solution)/shard_map/all_to_all | solution.py:265
  82.2 2.4 %fusion.7.other_ref = bf16[864,128]{1,0:T(8,128)(2,1)S(1)} fusion(bf16[864,5120]{1,0:T(8,128)(2,1)S(1)} %collective-permute-done.other_ref, bf16[16,8,5120]{2,1,0:T(8,128)(2,1)S(1)} %all_to_all.43), kind=kOutput, calls=%fused_computation.5 | convolution fusion | flops 1132572672 | bytes 10379264 | tf_op jit(solution)/shard_map/dot_general | solution.py:44
  84.7 2.4 %fusion.10.own_ref = bf16[864,128]{1,0:T(8,128)(2,1)S(1)} fusion(bf16[864,5120]{1,0:T(8,128)(2,1)S(1)} %bitcast.24, bf16[16,8,5120]{2,1,0:T(8,128)(2,1)S(1)} %all_to_all.43), kind=kOutput, calls=%fused_computation.6 | convolution fusion | flops 1132572672 | bytes 10379264 | tf_op jit(solution)/shard_map/dot_general | solution.py:44
  87.2 0.3 turn.1
  87.4 12.3 %all_to_all.44.grad_ref = bf16[16,8,1728]{2,1,0:T(8,128)(2,1)S(1)} all-to-all(bf16[16,8,1728]{2,1,0:T(8,128)(2,1)S(1)} %bitcast.28), channel_id=1, replica_groups=mesh['dp'=8,'chip_x'=4,'chip_y'=4,'core'=2] {'chip_x','chip_y'}, dimensions={0} | all-to-all | bytes 884736 | tf_op jit(solution)/shard_map/all_to_all | solution.py:265
  99.8 1.6 %backward.1 = bf16[32,40,256]{2,1,0:T(8,128)(2,1)S(1)} custom-call(bf16[16,8,1728]{2,1,0:T(8,128)(2,1)S(1)} %all_to_all.44.grad_ref, f32[2,1024,128]{2,1,0:T(8,128)S(1)} %get-tuple-element.28.slope_ref, f32[2,1024,128]{2,1,0:T(8,128)S(1)} %get-tuple-element.29.mixed_ref, bf16[1024,256]{1,0:T(8,128)(2,1)S(1)} %bitcast.27, ...), custom_call_target="tpu_custom_call" | custom-call | flops 530841600 | bytes 3096576 | tf_op jit(solution)/shard_map/backward/pallas_call | solution.py:343
  101.4 21.4 %all_to_all.45 = bf16[32,40,256]{2,1,0:T(8,128)(2,1)S(1)} all-to-all(bf16[32,40,256]{2,1,0:T(8,128)(2,1)S(1)} %backward.1), channel_id=1, replica_groups=mesh['dp'=8,'chip_x'=4,'chip_y'=4,'core'=2] {'chip_x','chip_y','core'}, dimensions={0} | all-to-all | bytes 1310720 | tf_op jit(solution)/shard_map/all_to_all | solution.py:265
  122.8 1.3 input_grad.1
  124.1 15.2 %all_to_all.46.parts_ref = f32[8,8,256]{2,1,0:T(8,128)S(1)} all-to-all(f32[8,8,256]{2,1,0:T(8,128)S(1)} %get-tuple-element.31), channel_id=1, replica_groups=mesh['dp'=8,'chip_x'=4,'chip_y'=4,'core'=2] {'dp'}, dimensions={0} | all-to-all | bytes 131072 | tf_op jit(solution)/shard_map/all_to_all | solution.py:265
  139.3 13.9 %all_to_all.47.parts_ref = f32[32,8,256]{2,1,0:T(8,128)S(1)} all-to-all(f32[32,8,256]{2,1,0:T(8,128)S(1)} %sum_and_copy.1), channel_id=1, replica_groups=mesh['dp'=8,'chip_x'=4,'chip_y'=4,'core'=2] {'chip_x','chip_y','core'}, dimensions={0} | all-to-all | bytes 524288 | tf_op jit(solution)/shard_map/all_to_all | solution.py:265
  153.2 0.8 unpack.1
  (2 shorter events, 0.0 us)
Async XLA Ops:
  0.6 21.7 %collective-permute-start = (bf16[864,5120]{1,0:T(8,128)(2,1)}, bf16[864,5120]{1,0:T(8,128)(2,1)S(1)}, u32[]{:S(2)}, u32[]{:S(2)}) collective-permute-start(bf16[864,5120]{1,0:T(8,128)(2,1)} %own_ref.1), channel_id=1, source_target_pairs={{0,1},{1,0},{2,3},{3,2},{4,5},{5,4},{6,7},{7,6},{8,9},{9,8},{10,11... | collective-permute-start | bytes 26542088 | tf_op jit(solution)/shard_map/ppermute | solution.py:277
  22.3 14.9 %slice-start = ((s8[8847360]{0:T(1024)(128)(4,1)}), s8[4194304]{0:T(1024)(128)(4,1)S(1)}, s32[]{:S(2)}) async-start(s8[8847360]{0:T(1024)(128)(4,1)} %bitcast.23), calls=%async_computation.8 | async-start | bytes 8388608
  22.3 14.9 %slice-start.1 = ((s8[8847360]{0:T(1024)(128)(4,1)}), s8[4194304]{0:T(1024)(128)(4,1)S(1)}, s32[]{:S(2)}) async-start(s8[8847360]{0:T(1024)(128)(4,1)} %bitcast.23), calls=%async_computation.9 | async-start | bytes 8388608
  22.3 14.9 %slice-start.2 = ((s8[8847360]{0:T(1024)(128)(4,1)}), s8[458752]{0:T(1024)(128)(4,1)S(1)}, s32[]{:S(2)}) async-start(s8[8847360]{0:T(1024)(128)(4,1)} %bitcast.23), calls=%async_computation.10 | async-start | bytes 917504

commit v6 on v5

--- a/solution.py
+++ b/solution.py
@@ -238,12 +238,13 @@
 
 
 def sum_and_copy_kernel(parts_ref, o_ref):
-    o_ref[...] = jnp.broadcast_to(jnp.sum(parts_ref[...], axis=0)[None], o_ref.shape)
+    total = jnp.sum(parts_ref[...], axis=0).astype(o_ref.dtype)
+    o_ref[...] = jnp.broadcast_to(total[None], o_ref.shape)
 
 
 def unpack_kernel(parts_ref, left_ref, right_ref):
     width, count = left_ref.shape[0], right_ref.shape[0]
-    packed = parts_ref[...].reshape(WIDE, WIDE)
+    packed = parts_ref[...].astype(F32).reshape(WIDE, WIDE)
     left_ref[...] = packed[:width, :width]
     low = WIDE - width
     right_ref[:low, :] = packed[width:, :count]
@@ -365,7 +366,7 @@
     )(back, back_left)
     factor_parts = exchange(factor_copies, "dp")
     factor_sums = call(
-        sum_and_copy_kernel, shape(owners, TOK, WIDE, dtype=F32), "sum_and_copy", 0, 1 << 20
+        sum_and_copy_kernel, shape(owners, TOK, WIDE), "sum_and_copy", 0, 1 << 20
     )(factor_parts)
     gathered = exchange(factor_sums, TENSOR)
     left_sum, right_sum = call(

time: 154 us -> 153 us (level)
  blocking collectives: 134 us -> 132 us
where the time goes in v6:
time: 153 us
  blocking collectives  132 us (86%)
  Pallas kernels  11.3 us (7%)
  matrix products  4.9 us (3%)
  starting transfers between devices  3.33 us (2%)
    all_to_all x8, blocking collectives, exchange(): return lax.all_to_all(array, axes, split_axis=0, concat_axis=0, tiled=True)  132 us
    dot_general x2, matrix products, dot(): return lax.dot_general(a, b, dims, preferred_element_type=F32)  4.9 us
    pallas_call x1, Pallas kernels, local(): call(project_kernel, (shape(half, columns), shape(2 * TOK, columns)), 'pr...  3.71 us
    ppermute x1, starting transfers between devices, local(): other_rows = lax.ppermute(weight_rows, 'core', [(0, 1), (1, 0)])  3.33 us
  transfers between devices with their start and end apart: 1, of which 0 were waited for; matrix products, arithmetic and copies ran while one was open for 0% of the time, Pallas kernels for 1%

profile of v6, /device:TPU:1, one launch (start us, length us, event | category | flops | bytes accessed | tf_op | source)
XLA Modules:
  0.0 152.7 jit_solution(7392379352135194133)
XLA Ops:
  0.6 3.3 %collective-permute-start = (bf16[864,5120]{1,0:T(8,128)(2,1)}, bf16[864,5120]{1,0:T(8,128)(2,1)S(1)}, u32[]{:S(2)}, u32[]{:S(2)}) collective-permute-start(bf16[864,5120]{1,0:T(8,128)(2,1)} %own_ref.1), channel_id=1, source_target_pairs={{0,1},{1,0},{2,3},{3,2},{4,5},{5,4},{6,7},{7,6},{8,9},{9,8},{10,11... | collective-permute-start | bytes 26542088 | tf_op jit(solution)/shard_map/ppermute | solution.py:278
  4.0 1.4 first.1
  5.4 16.9 %all_to_all.40 = bf16[32,32,256]{2,1,0:T(8,128)(2,1)S(1)} all-to-all(bf16[32,32,256]{2,1,0:T(8,128)(2,1)S(1)} %bitcast.30), channel_id=1, replica_groups=mesh['dp'=8,'chip_x'=4,'chip_y'=4,'core'=2] {'chip_x','chip_y','core'}, dimensions={0} | all-to-all | bytes 1048576 | tf_op jit(solution)/shard_map/all_to_all | solution.py:266
  22.3 0.0 collective-permute-done.other_ref
  22.3 0.0 slice-start
  22.3 0.0 slice-start.1
  22.3 0.0 slice-start.2
  22.3 2.0 %forward.1 = (bf16[16,8,1728]{2,1,0:T(8,128)(2,1)S(1)}, f32[2,1024,128]{2,1,0:T(8,128)S(1)}, f32[2,1024,128]{2,1,0:T(8,128)S(1)}) custom-call(bf16[1024,256]{1,0:T(8,128)(2,1)S(1)} %bitcast.26, bf16[256,512]{1,0:T(8,128)(2,1)S(1)} %get-tuple-element.21.left_ref, bf16[2,256,128]{2,1,0:T(8,128)(2,1)S(1)} %get-tuple-element.22.right_ref, ...), custom_call_target="tpu_custom_call" | custom-call | flops 10000000000 | bytes 2654208 | tf_op jit(solution)/shard_map/forward/pallas_call | solution.py:307
  24.4 12.8 %all_to_all.41.clip_ref = bf16[16,8,1728]{2,1,0:T(8,128)(2,1)S(1)} all-to-all(bf16[16,8,1728]{2,1,0:T(8,128)(2,1)S(1)} %get-tuple-element.24), channel_id=1, replica_groups=mesh['dp'=8,'chip_x'=4,'chip_y'=4,'core'=2] {'chip_x','chip_y'}, dimensions={0} | all-to-all | bytes 884736 | tf_op jit(solution)/shard_map/all_to_all | solution.py:266
  37.2 0.0 slice-done
  37.2 0.0 slice-done.1
  37.2 0.0 slice-done.2
  37.2 3.7 %project.1 = (bf16[128,5120]{1,0:T(8,128)(2,1)S(1)}, bf16[16,5120]{1,0:T(8,128)(2,1)S(1)}) custom-call(bf16[16,8,1728]{2,1,0:T(8,128)(2,1)S(1)} %all_to_all.41.clip_ref, bf16[864,5120]{1,0:T(8,128)(2,1)S(1)} %bitcast.24, bf16[864,5120]{1,0:T(8,128)(2,1)S(1)} %collective-permute-done.other_ref, bf16[256,5120]{1,0:T(8,128)(2,1)} %target_hbm.1), custom_call_target="tpu_custom_call" | custom-call | flops 2264924160 | bytes 17694720 | tf_op jit(solution)/shard_map/project/pallas_call | solution.py:316
  40.9 20.8 %all_to_all.42.parts_ref = bf16[16,8,5120]{2,1,0:T(8,128)(2,1)S(1)} all-to-all(bf16[16,8,5120]{2,1,0:T(8,128)(2,1)S(1)} %bitcast.29), channel_id=1, replica_groups=mesh['dp'=8,'chip_x'=4,'chip_y'=4,'core'=2] {'chip_x','chip_y'}, dimensions={0} | all-to-all | bytes 2621440 | tf_op jit(solution)/shard_map/all_to_all | solution.py:266
  61.7 0.2 residual.1
  62.0 20.3 %all_to_all.43 = bf16[16,8,5120]{2,1,0:T(8,128)(2,1)S(1)} all-to-all(bf16[16,8,5120]{2,1,0:T(8,128)(2,1)S(1)} %residual.1), channel_id=1, replica_groups=mesh['dp'=8,'chip_x'=4,'chip_y'=4,'core'=2] {'chip_x','chip_y'}, dimensions={0} | all-to-all | bytes 2621440 | tf_op jit(solution)/shard_map/all_to_all | solution.py:266
  82.2 2.4 %fusion.7.other_ref = bf16[864,128]{1,0:T(8,128)(2,1)S(1)} fusion(bf16[864,5120]{1,0:T(8,128)(2,1)S(1)} %collective-permute-done.other_ref, bf16[16,8,5120]{2,1,0:T(8,128)(2,1)S(1)} %all_to_all.43), kind=kOutput, calls=%fused_computation.5 | convolution fusion | flops 1132572672 | bytes 10379264 | tf_op jit(solution)/shard_map/dot_general | solution.py:44
  84.7 2.4 %fusion.10.own_ref = bf16[864,128]{1,0:T(8,128)(2,1)S(1)} fusion(bf16[864,5120]{1,0:T(8,128)(2,1)S(1)} %bitcast.24, bf16[16,8,5120]{2,1,0:T(8,128)(2,1)S(1)} %all_to_all.43), kind=kOutput, calls=%fused_computation.6 | convolution fusion | flops 1132572672 | bytes 10379264 | tf_op jit(solution)/shard_map/dot_general | solution.py:44
  87.2 0.3 turn.1
  87.4 12.3 %all_to_all.44.grad_ref = bf16[16,8,1728]{2,1,0:T(8,128)(2,1)S(1)} all-to-all(bf16[16,8,1728]{2,1,0:T(8,128)(2,1)S(1)} %bitcast.28), channel_id=1, replica_groups=mesh['dp'=8,'chip_x'=4,'chip_y'=4,'core'=2] {'chip_x','chip_y'}, dimensions={0} | all-to-all | bytes 884736 | tf_op jit(solution)/shard_map/all_to_all | solution.py:266
  99.8 1.6 %backward.1 = bf16[32,40,256]{2,1,0:T(8,128)(2,1)S(1)} custom-call(bf16[16,8,1728]{2,1,0:T(8,128)(2,1)S(1)} %all_to_all.44.grad_ref, f32[2,1024,128]{2,1,0:T(8,128)S(1)} %get-tuple-element.28.slope_ref, f32[2,1024,128]{2,1,0:T(8,128)S(1)} %get-tuple-element.29.mixed_ref, bf16[1024,256]{1,0:T(8,128)(2,1)S(1)} %bitcast.27, ...), custom_call_target="tpu_custom_call" | custom-call | flops 530841600 | bytes 3096576 | tf_op jit(solution)/shard_map/backward/pallas_call | solution.py:344
  101.4 21.4 %all_to_all.45 = bf16[32,40,256]{2,1,0:T(8,128)(2,1)S(1)} all-to-all(bf16[32,40,256]{2,1,0:T(8,128)(2,1)S(1)} %backward.1), channel_id=1, replica_groups=mesh['dp'=8,'chip_x'=4,'chip_y'=4,'core'=2] {'chip_x','chip_y','core'}, dimensions={0} | all-to-all | bytes 1310720 | tf_op jit(solution)/shard_map/all_to_all | solution.py:266
  122.8 1.3 input_grad.1
  124.1 15.2 %all_to_all.46.parts_ref = f32[8,8,256]{2,1,0:T(8,128)S(1)} all-to-all(f32[8,8,256]{2,1,0:T(8,128)S(1)} %get-tuple-element.31), channel_id=1, replica_groups=mesh['dp'=8,'chip_x'=4,'chip_y'=4,'core'=2] {'dp'}, dimensions={0} | all-to-all | bytes 131072 | tf_op jit(solution)/shard_map/all_to_all | solution.py:266
  139.3 12.6 %all_to_all.47.parts_ref = bf16[32,8,256]{2,1,0:T(8,128)(2,1)S(1)} all-to-all(bf16[32,8,256]{2,1,0:T(8,128)(2,1)S(1)} %sum_and_copy.1), channel_id=1, replica_groups=mesh['dp'=8,'chip_x'=4,'chip_y'=4,'core'=2] {'chip_x','chip_y','core'}, dimensions={0} | all-to-all | bytes 262144 | tf_op jit(solution)/shard_map/all_to_all | solution.py:266
  151.9 0.7 unpack.1
  (2 shorter events, 0.0 us)
Async XLA Ops:
  0.6 21.7 %collective-permute-start = (bf16[864,5120]{1,0:T(8,128)(2,1)}, bf16[864,5120]{1,0:T(8,128)(2,1)S(1)}, u32[]{:S(2)}, u32[]{:S(2)}) collective-permute-start(bf16[864,5120]{1,0:T(8,128)(2,1)} %own_ref.1), channel_id=1, source_target_pairs={{0,1},{1,0},{2,3},{3,2},{4,5},{5,4},{6,7},{7,6},{8,9},{9,8},{10,11... | collective-permute-start | bytes 26542088 | tf_op jit(solution)/shard_map/ppermute | solution.py:278
  22.3 14.9 %slice-start = ((s8[8847360]{0:T(1024)(128)(4,1)}), s8[4194304]{0:T(1024)(128)(4,1)S(1)}, s32[]{:S(2)}) async-start(s8[8847360]{0:T(1024)(128)(4,1)} %bitcast.23), calls=%async_computation.8 | async-start | bytes 8388608
  22.3 14.9 %slice-start.1 = ((s8[8847360]{0:T(1024)(128)(4,1)}), s8[4194304]{0:T(1024)(128)(4,1)S(1)}, s32[]{:S(2)}) async-start(s8[8847360]{0:T(1024)(128)(4,1)} %bitcast.23), calls=%async_computation.9 | async-start | bytes 8388608
  22.3 14.9 %slice-start.2 = ((s8[8847360]{0:T(1024)(128)(4,1)}), s8[458752]{0:T(1024)(128)(4,1)S(1)}, s32[]{:S(2)}) async-start(s8[8847360]{0:T(1024)(128)(4,1)} %bitcast.23), calls=%async_computation.10 | async-start | bytes 917504

commit v7 on v6

--- a/solution.py
+++ b/solution.py
@@ -217,7 +217,12 @@
     o_ref[:, own_rows:, :] = packed.reshape(owners, TOK, WIDE).astype(BF16)
 
 
-def input_grad_kernel(width, back_ref, left_ref, o_hbm, factor_ref, o_ref, sems):
+def plane_sum_kernel(back_ref, factor_ref):
+    factors = back_ref[:, -TOK:, :].astype(F32)
+    factor_ref[...] = jnp.broadcast_to(jnp.sum(factors, axis=0)[None], factor_ref.shape)
+
+
+def input_grad_kernel(width, back_ref, left_ref, o_hbm, o_ref, sems):
     chips, _, total, _ = back_ref.shape
     count = total // TOK - 1
     half = chips * TOK
@@ -231,8 +236,6 @@
         cut = pl.ds(j * width, width)
         copies.append(pltpu.make_async_copy(o_ref.at[cut], o_hbm.at[cut], sems.at[j]))
         copies[j].start()
-    factors = back_ref[:, :, count * TOK :, :].astype(F32)
-    factor_ref[...] = jnp.broadcast_to(jnp.sum(factors, axis=(0, 1))[None], factor_ref.shape)
     for copy in copies:
         copy.wait()
 
@@ -349,22 +352,25 @@
         14 * rows * width,
         scratch_shapes=[hold, hold],
     )(grad_owned, slope, mixed, moved, right_parts)
-    back = exchange(packed, TENSOR).reshape(chips, 2, per_owner, WIDE)
+    back = exchange(packed, TENSOR)
 
     groups = lax.axis_size("dp")
-    input_grad, factor_copies = call(
+    factor_copies = call(
+        plane_sum_kernel, shape(groups, TOK, WIDE, dtype=F32), "plane_sum", 0, 1 << 18
+    )(back)
+    factor_parts = exchange(factor_copies, "dp")
+    input_grad = call(
         functools.partial(input_grad_kernel, width),
-        (shape(hidden, tokens, dtype=F32), shape(groups, TOK, WIDE, dtype=F32)),
+        shape(hidden, tokens, dtype=F32),
         "input_grad",
         4 * tokens * hidden * width,
         6 * tokens * hidden,
-        out_specs=(pl.BlockSpec(memory_space=HBM), pl.BlockSpec()),
+        out_specs=pl.BlockSpec(memory_space=HBM),
         scratch_shapes=[
             pltpu.VMEM((hidden, tokens), F32),
             pltpu.SemaphoreType.DMA((each,)),
         ],
-    )(back, back_left)
-    factor_parts = exchange(factor_copies, "dp")
+    )(back.reshape(chips, 2, per_owner, WIDE), back_left)
     factor_sums = call(
         sum_and_copy_kernel, shape(owners, TOK, WIDE), "sum_and_copy", 0, 1 << 20
     )(factor_parts)

time: 153 us -> 153 us (level)
  blocking collectives: 132 us -> 120 us
  waiting for transfers between devices: 0.01 us -> 6.45 us
  starting transfers between devices: 3.33 us -> 8.42 us
    all_to_all x8 -> x7, blocking collectives: 132 us -> 120 us  [exchange(): return lax.all_to_all(array, axes, split_axis=0, concat_axis=0, tiled=True)]
    all_to_all x0 -> x1, waiting for transfers between devices: none -> 6.45 us  [exchange(): return lax.all_to_all(array, axes, split_axis=0, concat_axis=0, tiled=True)]
    all_to_all x0 -> x1, starting transfers between devices: none -> 5.09 us  [exchange(): return lax.all_to_all(array, axes, split_axis=0, concat_axis=0, tiled=True)]
  transfers between devices with their start and end apart: 1 -> 2, of which waited for: 0 -> 1; matrix products, arithmetic and copies ran while one was open for 0% -> 0% of each run, Pallas kernels for 1% -> 2%
where the time goes in v7:
time: 153 us; the launch traced here: 152 us
  blocking collectives  120 us (78%)
  Pallas kernels  12 us (8%)
  starting transfers between devices  8.42 us (6%)
  waiting for transfers between devices  6.45 us (4%)
  matrix products  4.9 us (3%)
    all_to_all x7, blocking collectives, exchange(): return lax.all_to_all(array, axes, split_axis=0, concat_axis=0, tiled=True)  120 us
    all_to_all x1, waiting for transfers between devices, exchange(): return lax.all_to_all(array, axes, split_axis=0, concat_axis=0, tiled=True)  6.45 us
    all_to_all x1, starting transfers between devices, exchange(): return lax.all_to_all(array, axes, split_axis=0, concat_axis=0, tiled=True)  5.09 us
    dot_general x2, matrix products, dot(): return lax.dot_general(a, b, dims, preferred_element_type=F32)  4.9 us
    pallas_call x1, Pallas kernels, local(): call(project_kernel, (shape(half, columns), shape(2 * TOK, columns)), 'pr...  3.72 us
    ppermute x1, starting transfers between devices, local(): other_rows = lax.ppermute(weight_rows, 'core', [(0, 1), (1, 0)])  3.33 us
  transfers between devices with their start and end apart: 2, of which 1 were waited for; matrix products, arithmetic and copies ran while one was open for 0% of the time, Pallas kernels for 2%

profile of v7, /device:TPU:1, one launch (start us, length us, event | category | flops | bytes accessed | tf_op | source)
XLA Modules:
  0.0 152.3 jit_solution(10788777818389208814)
XLA Ops:
  0.6 3.3 %collective-permute-start = (bf16[864,5120]{1,0:T(8,128)(2,1)}, bf16[864,5120]{1,0:T(8,128)(2,1)S(1)}, u32[]{:S(2)}, u32[]{:S(2)}) collective-permute-start(bf16[864,5120]{1,0:T(8,128)(2,1)} %own_ref.1), channel_id=1, source_target_pairs={{0,1},{1,0},{2,3},{3,2},{4,5},{5,4},{6,7},{7,6},{8,9},{9,8},{10,11... | collective-permute-start | bytes 26542088 | tf_op jit(solution)/shard_map/ppermute | solution.py:281
  4.0 1.4 first.1
  5.4 16.9 %all_to_all.40 = bf16[32,32,256]{2,1,0:T(8,128)(2,1)S(1)} all-to-all(bf16[32,32,256]{2,1,0:T(8,128)(2,1)S(1)} %bitcast.30), channel_id=1, replica_groups=mesh['dp'=8,'chip_x'=4,'chip_y'=4,'core'=2] {'chip_x','chip_y','core'}, dimensions={0} | all-to-all | bytes 1048576 | tf_op jit(solution)/shard_map/all_to_all | solution.py:269
  22.3 0.0 collective-permute-done.other_ref
  22.3 0.0 slice-start
  22.3 0.0 slice-start.1
  22.3 0.0 slice-start.2
  22.3 2.0 %forward.1 = (bf16[16,8,1728]{2,1,0:T(8,128)(2,1)S(1)}, f32[2,1024,128]{2,1,0:T(8,128)S(1)}, f32[2,1024,128]{2,1,0:T(8,128)S(1)}) custom-call(bf16[1024,256]{1,0:T(8,128)(2,1)S(1)} %bitcast.26, bf16[256,512]{1,0:T(8,128)(2,1)S(1)} %get-tuple-element.19.left_ref, bf16[2,256,128]{2,1,0:T(8,128)(2,1)S(1)} %get-tuple-element.20.right_ref, ...), custom_call_target="tpu_custom_call" | custom-call | flops 10000000000 | bytes 2654208 | tf_op jit(solution)/shard_map/forward/pallas_call | solution.py:310
  24.4 12.8 %all_to_all.41.clip_ref = bf16[16,8,1728]{2,1,0:T(8,128)(2,1)S(1)} all-to-all(bf16[16,8,1728]{2,1,0:T(8,128)(2,1)S(1)} %get-tuple-element.22), channel_id=1, replica_groups=mesh['dp'=8,'chip_x'=4,'chip_y'=4,'core'=2] {'chip_x','chip_y'}, dimensions={0} | all-to-all | bytes 884736 | tf_op jit(solution)/shard_map/all_to_all | solution.py:269
  37.2 0.0 slice-done
  37.2 0.0 slice-done.1
  37.2 0.0 slice-done.2
  37.2 3.7 %project.1 = (bf16[128,5120]{1,0:T(8,128)(2,1)S(1)}, bf16[16,5120]{1,0:T(8,128)(2,1)S(1)}) custom-call(bf16[16,8,1728]{2,1,0:T(8,128)(2,1)S(1)} %all_to_all.41.clip_ref, bf16[864,5120]{1,0:T(8,128)(2,1)S(1)} %bitcast.24, bf16[864,5120]{1,0:T(8,128)(2,1)S(1)} %collective-permute-done.other_ref, bf16[256,5120]{1,0:T(8,128)(2,1)} %target_hbm.1), custom_call_target="tpu_custom_call" | custom-call | flops 2264924160 | bytes 17694720 | tf_op jit(solution)/shard_map/project/pallas_call | solution.py:319
  41.0 20.8 %all_to_all.42.parts_ref = bf16[16,8,5120]{2,1,0:T(8,128)(2,1)S(1)} all-to-all(bf16[16,8,5120]{2,1,0:T(8,128)(2,1)S(1)} %bitcast.29), channel_id=1, replica_groups=mesh['dp'=8,'chip_x'=4,'chip_y'=4,'core'=2] {'chip_x','chip_y'}, dimensions={0} | all-to-all | bytes 2621440 | tf_op jit(solution)/shard_map/all_to_all | solution.py:269
  61.7 0.2 residual.1
  62.0 20.3 %all_to_all.43 = bf16[16,8,5120]{2,1,0:T(8,128)(2,1)S(1)} all-to-all(bf16[16,8,5120]{2,1,0:T(8,128)(2,1)S(1)} %residual.1), channel_id=1, replica_groups=mesh['dp'=8,'chip_x'=4,'chip_y'=4,'core'=2] {'chip_x','chip_y'}, dimensions={0} | all-to-all | bytes 2621440 | tf_op jit(solution)/shard_map/all_to_all | solution.py:269
  82.2 2.4 %fusion.7.other_ref = bf16[864,128]{1,0:T(8,128)(2,1)S(1)} fusion(bf16[864,5120]{1,0:T(8,128)(2,1)S(1)} %collective-permute-done.other_ref, bf16[16,8,5120]{2,1,0:T(8,128)(2,1)S(1)} %all_to_all.43), kind=kOutput, calls=%fused_computation.5 | convolution fusion | flops 1132572672 | bytes 10379264 | tf_op jit(solution)/shard_map/dot_general | solution.py:44
  84.7 2.5 %fusion.10.own_ref = bf16[864,128]{1,0:T(8,128)(2,1)S(1)} fusion(bf16[864,5120]{1,0:T(8,128)(2,1)S(1)} %bitcast.24, bf16[16,8,5120]{2,1,0:T(8,128)(2,1)S(1)} %all_to_all.43), kind=kOutput, calls=%fused_computation.6 | convolution fusion | flops 1132572672 | bytes 10379264 | tf_op jit(solution)/shard_map/dot_general | solution.py:44
  87.2 0.3 turn.1
  87.4 12.3 %all_to_all.44.grad_ref = bf16[16,8,1728]{2,1,0:T(8,128)(2,1)S(1)} all-to-all(bf16[16,8,1728]{2,1,0:T(8,128)(2,1)S(1)} %bitcast.28), channel_id=1, replica_groups=mesh['dp'=8,'chip_x'=4,'chip_y'=4,'core'=2] {'chip_x','chip_y'}, dimensions={0} | all-to-all | bytes 884736 | tf_op jit(solution)/shard_map/all_to_all | solution.py:269
  99.7 1.6 %backward.1 = bf16[32,40,256]{2,1,0:T(8,128)(2,1)S(1)} custom-call(bf16[16,8,1728]{2,1,0:T(8,128)(2,1)S(1)} %all_to_all.44.grad_ref, f32[2,1024,128]{2,1,0:T(8,128)S(1)} %get-tuple-element.26.slope_ref, f32[2,1024,128]{2,1,0:T(8,128)S(1)} %get-tuple-element.27.mixed_ref, bf16[1024,256]{1,0:T(8,128)(2,1)S(1)} %bitcast.27, ...), custom_call_target="tpu_custom_call" | custom-call | flops 530841600 | bytes 3096576 | tf_op jit(solution)/shard_map/backward/pallas_call | solution.py:347
  101.3 21.5 %all_to_all.45.back_ref = bf16[32,40,256]{2,1,0:T(8,128)(2,1)S(1)} all-to-all(bf16[32,40,256]{2,1,0:T(8,128)(2,1)S(1)} %backward.1), channel_id=1, replica_groups=mesh['dp'=8,'chip_x'=4,'chip_y'=4,'core'=2] {'chip_x','chip_y','core'}, dimensions={0} | all-to-all | bytes 1310720 | tf_op jit(solution)/shard_map/all_to_all | solution.py:269
  122.8 15.2 %all_to_all.46.parts_ref = f32[8,8,256]{2,1,0:T(8,128)S(1)} all-to-all(f32[8,8,256]{2,1,0:T(8,128)S(1)} %plane_sum.1), channel_id=1, replica_groups=mesh['dp'=8,'chip_x'=4,'chip_y'=4,'core'=2] {'dp'}, dimensions={0} | all-to-all | bytes 131072 | tf_op jit(solution)/shard_map/all_to_all | solution.py:269
  138.1 0.7 sum_and_copy.1
  138.7 5.1 %all-to-all-start.7 = ((bf16[32,8,256]{2,1,0:T(8,128)(2,1)}), bf16[32,8,256]{2,1,0:T(8,128)(2,1)S(1)}, u32[]{:S(2)}, u32[]{:S(2)}) async-start(bf16[32,8,256]{2,1,0:T(8,128)(2,1)} %sum_and_copy.1), calls=%async_computation.7 | async-start | bytes 262144 | tf_op jit(solution)/shard_map/all_to_all | solution.py:269
  143.8 1.2 input_grad.1
  145.1 6.4 %all-to-all-done.7.parts_ref = bf16[32,8,256]{2,1,0:T(8,128)(2,1)S(1)} async-done(((bf16[32,8,256]{2,1,0:T(8,128)(2,1)}), bf16[32,8,256]{2,1,0:T(8,128)(2,1)S(1)}, u32[]{:S(2)}, u32[]{:S(2)}) %all-to-all-start.7) | async-done | bytes 131104 | tf_op jit(solution)/shard_map/all_to_all | solution.py:269
  151.5 0.7 unpack.1
  (2 shorter events, 0.0 us)
Async XLA Ops:
  0.6 21.7 %collective-permute-start = (bf16[864,5120]{1,0:T(8,128)(2,1)}, bf16[864,5120]{1,0:T(8,128)(2,1)S(1)}, u32[]{:S(2)}, u32[]{:S(2)}) collective-permute-start(bf16[864,5120]{1,0:T(8,128)(2,1)} %own_ref.1), channel_id=1, source_target_pairs={{0,1},{1,0},{2,3},{3,2},{4,5},{5,4},{6,7},{7,6},{8,9},{9,8},{10,11... | collective-permute-start | bytes 26542088 | tf_op jit(solution)/shard_map/ppermute | solution.py:281
  22.3 14.9 %slice-start = ((s8[8847360]{0:T(1024)(128)(4,1)}), s8[4194304]{0:T(1024)(128)(4,1)S(1)}, s32[]{:S(2)}) async-start(s8[8847360]{0:T(1024)(128)(4,1)} %bitcast.23), calls=%async_computation.8 | async-start | bytes 8388608
  22.3 14.9 %slice-start.1 = ((s8[8847360]{0:T(1024)(128)(4,1)}), s8[4194304]{0:T(1024)(128)(4,1)S(1)}, s32[]{:S(2)}) async-start(s8[8847360]{0:T(1024)(128)(4,1)} %bitcast.23), calls=%async_computation.9 | async-start | bytes 8388608
  22.3 14.9 %slice-start.2 = ((s8[8847360]{0:T(1024)(128)(4,1)}), s8[458752]{0:T(1024)(128)(4,1)S(1)}, s32[]{:S(2)}) async-start(s8[8847360]{0:T(1024)(128)(4,1)} %bitcast.23), calls=%async_computation.10 | async-start | bytes 917504
  138.7 12.8 %all-to-all-start.7 = ((bf16[32,8,256]{2,1,0:T(8,128)(2,1)}), bf16[32,8,256]{2,1,0:T(8,128)(2,1)S(1)}, u32[]{:S(2)}, u32[]{:S(2)}) async-start(bf16[32,8,256]{2,1,0:T(8,128)(2,1)} %sum_and_copy.1), calls=%async_computation.7 | async-start | bytes 262144 | tf_op jit(solution)/shard_map/all_to_all | solution.py:269
